TPU v7x, 32 devices: a whole 2x2x4 slice. The times are simulated.
32 devices in a mesh: dp: 16 (over z, x, core), tensor: 2 (over y).
Axes of the slice: x: 2, y: 2, z: 4, core: 2. Of those that a mesh axis runs over, the one named last changes fastest.
Arguments:
- tokens: bfloat16 [32, 512, 768], P('dp', 'tensor'), may hold values from -6 to 6
- cotangent: bfloat16 [32, 512, 768], P('dp', 'tensor'), may hold values from -6 to 6
- lengths: int32 [32], replicated, may hold values from 1 to 512, 10240 in all
- slot_order: int32 [32], replicated, may hold values from 0 to 31, each once
- query_weight: bfloat16 [768, 768], P('dp', 'tensor'), may hold values from -0.21875 to 0.21875
- key_weight: bfloat16 [768, 768], P('dp', 'tensor'), may hold values from -0.21875 to 0.21875
- value_weight: bfloat16 [768, 768], P('dp', 'tensor'), may hold values from -0.21875 to 0.21875
- out_weight: bfloat16 [768, 768], P('dp', 'tensor'), may hold values from -1.5 to 1.5
- up_weight: bfloat16 [768, 3072], P('dp', 'tensor'), may hold values from -0.21875 to 0.21875
- down_weight: bfloat16 [768, 3072], P('dp', 'tensor'), may hold values from -0.109375 to 0.109375
- query_bias: float32 [768], P('tensor'), may hold values from -3 to 3
- value_bias: float32 [768], P('tensor'), may hold values from -0.3 to 0.3
- out_bias: float32 [768], replicated, may hold values from -3 to 3
- up_bias: float32 [3072], P('tensor'), may hold values from -3 to 3
- down_bias: float32 [768], replicated, may hold values from -3 to 3
- first_gain: float32 [768], replicated, may hold values from 0.5 to 1.5
- first_offset: float32 [768], replicated, may hold values from -3 to 3
- second_gain: float32 [768], replicated, may hold values from 0.5 to 1.5
- second_offset: float32 [768], replicated, may hold values from -3 to 3
Outputs:
- layer_out: bfloat16 [32, 512, 768], P('dp', 'tensor')
- input_grad: bfloat16 [32, 512, 768], P('dp', 'tensor')
- query_weight_grad: float32 [768, 768], P('dp', 'tensor')
- key_weight_grad: float32 [768, 768], P('dp', 'tensor')
- value_weight_grad: float32 [768, 768], P('dp', 'tensor')
- out_weight_grad: float32 [768, 768], P('dp', 'tensor')
- up_weight_grad: float32 [768, 3072], P('dp', 'tensor')
- down_weight_grad: float32 [768, 3072], P('dp', 'tensor')
- query_bias_grad: float32 [768], P('tensor')
- value_bias_grad: float32 [768], P('tensor')
- out_bias_grad: float32 [768], replicated
- up_bias_grad: float32 [3072], P('tensor')
- down_bias_grad: float32 [768], replicated
- first_gain_grad: float32 [768], replicated
- first_offset_grad: float32 [768], replicated
- second_gain_grad: float32 [768], replicated
- second_offset_grad: float32 [768], replicated
Inputs may be any that keep to these rules, and one draw needn't show every extreme that they name: The lengths of the 32 sequences sum to 10240, and the longest is exactly 512. `slot_order`: every sequence is held by exactly one slot.
All inputs are finite; a program needn't handle non-finite values.
Results may differ from a plain program's by a relative error of at most 0.017.
Values may be sent and summed in bfloat16 or wider, within the bound.
No kernel may reach another device: no remote copies, remote signals or barrier semaphores. Data moves between devices by JAX's collectives and lax.ppermute only.
A program may use at most 128 MiB of HBM per device.

v0:
```python
import jax
import jax.numpy as jnp
from jax import lax
from jax.sharding import PartitionSpec as P

HEAD = 64


EPSILON = 1e-05
SQRT_HALF = 0.7071067811865476
INV_ROOT_TWO_PI = 0.3989422804014327


def norm_forward(inputs, norm_gain, offset):
    center = inputs - jnp.mean(inputs, axis=-1, keepdims=True)
    rscale = lax.rsqrt(jnp.mean(center * center, axis=-1, keepdims=True) + EPSILON)
    normal = center * rscale
    return (normal * norm_gain + offset, normal, rscale)


def norm_backward(incoming, normal, rscale, norm_gain):
    scaled = incoming * norm_gain
    inner_term = (
        scaled
        - jnp.mean(scaled, axis=-1, keepdims=True)
        - normal * jnp.mean(scaled * normal, axis=-1, keepdims=True)
    )
    return (rscale * inner_term, jnp.sum(incoming * normal, axis=0), jnp.sum(incoming, axis=0))


def gelu_exact(inputs):
    return 0.5 * inputs * (1.0 + lax.erf(inputs * SQRT_HALF))


def gelu_slope(inputs):
    return (
        0.5 * (1.0 + lax.erf(inputs * SQRT_HALF))
        + inputs * jnp.exp(-0.5 * inputs * inputs) * INV_ROOT_TWO_PI
    )


def contract_rows(left_side, right_side):
    return lax.dot_general(
        left_side, right_side, (((0,), (0,)), ((), ())), preferred_element_type=jnp.float32
    )


def contract_cols(left_side, right_side):
    return lax.dot_general(
        left_side, right_side, (((1,), (1,)), ((), ())), preferred_element_type=jnp.float32
    )


def deal_rows(seq_block, row_order):
    micro_count, row_count, features = seq_block.shape
    flattened = seq_block.reshape(micro_count, row_count * features)
    spread = lax.all_to_all(flattened, "dp", split_axis=1, concat_axis=0, tiled=True)
    chosen = jnp.take(spread, row_order, axis=0)
    joined = lax.all_to_all(chosen, "dp", split_axis=0, concat_axis=1, tiled=True)
    return joined.reshape(micro_count, row_count, features)


def on_device(
    tokens,
    cotangent,
    lengths,
    slot_order,
    query_weight,
    key_weight,
    value_weight,
    out_weight,
    up_weight,
    down_weight,
    query_bias,
    value_bias,
    out_bias,
    up_bias,
    down_bias,
    first_gain,
    first_offset,
    second_gain,
    second_offset,
):
    micro_count, row_count, features = tokens.shape
    tensor_size = lax.axis_size("tensor")
    tensor_pos = lax.axis_index("tensor")
    dp_pos = lax.axis_index("dp")
    seq_len = row_count * tensor_size
    head_cols = query_weight.shape[1]
    unit_cols = up_weight.shape[1]
    head_count = head_cols // HEAD
    block_rows = min(512, seq_len)
    score_scale = HEAD ** (-0.5)
    slot_count = slot_order.shape[0]
    inverse = jnp.zeros_like(slot_order).at[slot_order].set(jnp.arange(slot_count, dtype=jnp.int32))
    slot_lens = lax.dynamic_slice_in_dim(
        jnp.take(lengths, slot_order), dp_pos * micro_count, micro_count
    )
    dealt = deal_rows(tokens, slot_order)
    positions = jnp.arange(seq_len, dtype=jnp.int32)
    own_rows = tensor_pos * row_count + jnp.arange(row_count, dtype=jnp.int32)
    acc_query = jnp.zeros((features, head_cols), jnp.float32)
    acc_key = jnp.zeros((features, head_cols), jnp.float32)
    acc_value = jnp.zeros((features, head_cols), jnp.float32)
    acc_out = jnp.zeros((features, head_cols), jnp.float32)
    acc_up = jnp.zeros((features, unit_cols), jnp.float32)
    acc_down = jnp.zeros((features, unit_cols), jnp.float32)
    sum_qbias = jnp.zeros((head_cols,), jnp.float32)
    sum_vbias = jnp.zeros((head_cols,), jnp.float32)
    sum_ubias = jnp.zeros((unit_cols,), jnp.float32)
    sum_vectors = jnp.zeros((6, features), jnp.float32)
    layer_rows, grad_rows = ([], [])
    for micro_step in range(micro_count):
        weights = (
            lax.all_gather(query_weight, "dp", axis=0, tiled=True),
            lax.all_gather(key_weight, "dp", axis=0, tiled=True),
            lax.all_gather(value_weight, "dp", axis=0, tiled=True),
            lax.all_gather(out_weight, "dp", axis=0, tiled=True),
            lax.all_gather(up_weight, "dp", axis=0, tiled=True),
            lax.all_gather(down_weight, "dp", axis=0, tiled=True),
        )
        query_full, key_full, value_full, out_full, up_full, down_full = weights
        live_len = slot_lens[micro_step]
        key_live = positions < live_len
        row_live = (own_rows < live_len).astype(jnp.float32)[:, None]
        own_tokens = dealt[micro_step]
        full_tokens = lax.all_gather(own_tokens, "tensor", axis=0, tiled=True)
        split_shape = (seq_len, head_count, HEAD)
        queries = (
            (jnp.dot(full_tokens, query_full, preferred_element_type=jnp.float32) + query_bias)
            .astype(jnp.bfloat16)
            .reshape(split_shape)
        )
        key_rows = (
            jnp.dot(full_tokens, key_full, preferred_element_type=jnp.float32)
            .astype(jnp.bfloat16)
            .reshape(split_shape)
        )
        values = (
            (jnp.dot(full_tokens, value_full, preferred_element_type=jnp.float32) + value_bias)
            .astype(jnp.bfloat16)
            .reshape(split_shape)
        )
        attend_scores = (
            jnp.einsum("qhd,khd->hqk", queries, key_rows, preferred_element_type=jnp.float32)
            * score_scale
        )
        attend_scores = jnp.where(key_live[None, None, :], attend_scores, -1000000000.0)
        row_max = jnp.max(attend_scores, axis=-1, keepdims=True)
        raised = jnp.exp(attend_scores - row_max)
        row_total = jnp.sum(raised, axis=-1, keepdims=True)
        attend_attn_probs = (raised / row_total).astype(jnp.bfloat16)
        mixed = jnp.einsum(
            "hqk,khd->qhd", attend_attn_probs, values, preferred_element_type=jnp.float32
        )
        outputs = mixed.astype(jnp.bfloat16)
        attend_log_totals = [(row_max + jnp.log(row_total))[:, :, 0]]
        attended_flat = outputs.reshape(seq_len, head_cols)
        attn_out = (
            lax.psum_scatter(
                contract_cols(attended_flat, out_full).astype(jnp.bfloat16),
                "tensor",
                scatter_dimension=0,
                tiled=True,
            ).astype(jnp.float32)
            + out_bias
        )
        normed, normal_one, rscale_one = norm_forward(
            own_tokens.astype(jnp.float32) + attn_out, first_gain, first_offset
        )
        normed_full = lax.all_gather(normed.astype(jnp.bfloat16), "tensor", axis=0, tiled=True)
        hidden = jnp.dot(normed_full, up_full, preferred_element_type=jnp.float32) + up_bias
        act_low = gelu_exact(hidden).astype(jnp.bfloat16)
        ffn_out = (
            lax.psum_scatter(
                contract_cols(act_low, down_full).astype(jnp.bfloat16),
                "tensor",
                scatter_dimension=0,
                tiled=True,
            ).astype(jnp.float32)
            + down_bias
        )
        final_norm, normal_two, rscale_two = norm_forward(
            normed + ffn_out, second_gain, second_offset
        )
        layer_rows.append((final_norm * row_live).astype(jnp.bfloat16))
        grad_out = cotangent[micro_step].astype(jnp.float32) * row_live
        grad_second, gain_two, offset_two = norm_backward(
            grad_out, normal_two, rscale_two, second_gain
        )
        grad_ffn_low = grad_second.astype(jnp.bfloat16)
        grad_ffn_full = lax.all_gather(grad_ffn_low, "tensor", axis=0, tiled=True)
        grad_act = jnp.dot(grad_ffn_full, down_full, preferred_element_type=jnp.float32)
        grad_hidden_low = (grad_act * gelu_slope(hidden)).astype(jnp.bfloat16)
        grad_normed = (
            lax.psum_scatter(
                contract_cols(grad_hidden_low, up_full).astype(jnp.bfloat16),
                "tensor",
                scatter_dimension=0,
                tiled=True,
            ).astype(jnp.float32)
            + grad_second
        )
        grad_first, gain_one, offset_one = norm_backward(
            grad_normed, normal_one, rscale_one, first_gain
        )
        grad_attn_low = grad_first.astype(jnp.bfloat16)
        grad_attn_full = lax.all_gather(grad_attn_low, "tensor", axis=0, tiled=True)
        grad_attended = (
            jnp.dot(grad_attn_full, out_full, preferred_element_type=jnp.float32)
            .astype(jnp.bfloat16)
            .reshape(split_shape)
        )
        query_parts = []
        grad_keys = jnp.zeros((seq_len, head_count, HEAD), jnp.float32)
        grad_values = jnp.zeros((seq_len, head_count, HEAD), jnp.float32)
        for block_pos, row_start in enumerate(range(0, seq_len, block_rows)):
            log_total = attend_log_totals[block_pos]
            scores = (
                jnp.einsum("qhd,khd->hqk", queries, key_rows, preferred_element_type=jnp.float32)
                * score_scale
            )
            scores = jnp.where(key_live[None, None, :], scores, -1000000000.0)
            attn_probs = jnp.exp(scores - log_total[:, :, None])
            grad_probs = jnp.einsum(
                "qhd,khd->hqk", grad_attended, values, preferred_element_type=jnp.float32
            )
            row_inner = jnp.sum(grad_probs * attn_probs, axis=-1, keepdims=True)
            grad_scores = (attn_probs * (grad_probs - row_inner) * score_scale).astype(jnp.bfloat16)
            query_parts.append(
                jnp.einsum(
                    "hqk,khd->qhd", grad_scores, key_rows, preferred_element_type=jnp.float32
                )
            )
            grad_keys = jnp.einsum(
                "hqk,qhd->khd", grad_scores, queries, preferred_element_type=jnp.float32
            )
            grad_values = jnp.einsum(
                "hqk,qhd->khd",
                attn_probs.astype(jnp.bfloat16),
                grad_attended,
                preferred_element_type=jnp.float32,
            )
        grad_queries, grad_keys, grad_values = (query_parts[0], grad_keys, grad_values)
        query_grad_low = grad_queries.astype(jnp.bfloat16).reshape(seq_len, head_cols)
        key_grad_low = grad_keys.astype(jnp.bfloat16).reshape(seq_len, head_cols)
        value_grad_low = grad_values.astype(jnp.bfloat16).reshape(seq_len, head_cols)
        token_terms = (
            contract_cols(query_grad_low, query_full)
            + contract_cols(key_grad_low, key_full)
            + contract_cols(value_grad_low, value_full)
        )
        grad_tokens = (
            lax.psum_scatter(
                token_terms.astype(jnp.bfloat16), "tensor", scatter_dimension=0, tiled=True
            ).astype(jnp.float32)
            + grad_first
        )
        grad_rows.append(grad_tokens.astype(jnp.bfloat16))
        acc_query = acc_query + contract_rows(full_tokens, query_grad_low)
        acc_key = acc_key + contract_rows(full_tokens, key_grad_low)
        acc_value = acc_value + contract_rows(full_tokens, value_grad_low)
        acc_out = acc_out + contract_rows(grad_attn_full, attended_flat)
        acc_up = acc_up + contract_rows(normed_full, grad_hidden_low)
        acc_down = acc_down + contract_rows(grad_ffn_full, act_low)
        sum_qbias = sum_qbias + jnp.sum(query_grad_low.astype(jnp.float32), axis=0)
        sum_vbias = sum_vbias + jnp.sum(value_grad_low.astype(jnp.float32), axis=0)
        sum_ubias = sum_ubias + jnp.sum(grad_hidden_low.astype(jnp.float32), axis=0)
        sum_vectors = sum_vectors + jnp.stack(
            [
                jnp.sum(grad_attn_low.astype(jnp.float32), axis=0),
                gain_one,
                offset_one,
                jnp.sum(grad_ffn_low.astype(jnp.float32), axis=0),
                gain_two,
                offset_two,
            ]
        )
    layer_out = jnp.stack(layer_rows)
    input_grad = deal_rows(jnp.stack(grad_rows), inverse)
    weight_sums = (
        lax.psum_scatter(acc_query, "dp", scatter_dimension=0, tiled=True),
        lax.psum_scatter(acc_key, "dp", scatter_dimension=0, tiled=True),
        lax.psum_scatter(acc_value, "dp", scatter_dimension=0, tiled=True),
        lax.psum_scatter(acc_out, "dp", scatter_dimension=0, tiled=True),
        lax.psum_scatter(acc_up, "dp", scatter_dimension=0, tiled=True),
        lax.psum_scatter(acc_down, "dp", scatter_dimension=0, tiled=True),
    )
    onehot = (jnp.arange(tensor_size, dtype=jnp.int32) == tensor_pos).astype(jnp.float32)

    def place_part(part_vec):
        return (onehot[:, None] * part_vec[None, :]).reshape(-1)

    vector_sums, head_sums, unit_sums = lax.psum(
        (
            sum_vectors,
            jnp.stack([place_part(sum_qbias), place_part(sum_vbias)]),
            place_part(sum_ubias),
        ),
        ("dp", "tensor"),
    )
    query_bias_grad = lax.dynamic_slice_in_dim(head_sums[0], tensor_pos * head_cols, head_cols)
    value_bias_grad = lax.dynamic_slice_in_dim(head_sums[1], tensor_pos * head_cols, head_cols)
    up_bias_grad = lax.dynamic_slice_in_dim(unit_sums, tensor_pos * unit_cols, unit_cols)
    return (
        layer_out,
        input_grad,
        weight_sums[0],
        weight_sums[1],
        weight_sums[2],
        weight_sums[3],
        weight_sums[4],
        weight_sums[5],
        query_bias_grad,
        value_bias_grad,
        vector_sums[0],
        up_bias_grad,
        vector_sums[3],
        vector_sums[1],
        vector_sums[2],
        vector_sums[4],
        vector_sums[5],
    )


def solution(mesh):
    placed = (
        P("dp", "tensor", None),
        P("dp", "tensor", None),
        P(),
        P(),
        P("dp", "tensor"),
        P("dp", "tensor"),
        P("dp", "tensor"),
        P("dp", "tensor"),
        P("dp", "tensor"),
        P("dp", "tensor"),
        P("tensor"),
        P("tensor"),
        P(),
        P("tensor"),
        P(),
        P(),
        P(),
        P(),
        P(),
    )
    return jax.shard_map(
        on_device,
        mesh=mesh,
        in_specs=placed,
        out_specs=(
            P("dp", "tensor", None),
            P("dp", "tensor", None),
            P("dp", "tensor"),
            P("dp", "tensor"),
            P("dp", "tensor"),
            P("dp", "tensor"),
            P("dp", "tensor"),
            P("dp", "tensor"),
            P("tensor"),
            P("tensor"),
            P(),
            P("tensor"),
            P(),
            P(),
            P(),
            P(),
            P(),
        ),
        check_vma=False,
    )
```

profile of v0, /device:TPU:0, one launch (start us, length us, event | category | flops | bytes accessed | tf_op | source)
XLA Modules:
  0.0 928.7 jit_solution(2102585400114085130)
XLA Ops:
  19.9 17.4 %all-to-all-done = bf16[2,16,12288]{2,0,1:T(2,128)(2,1)S(1)} async-done(((bf16[2,16,12288]{2,0,1:T(2,128)(2,1)}), bf16[2,16,12288]{2,0,1:T(2,128)(2,1)S(1)}, u32[]{:S(2)}, u32[]{:S(2)}) %all-to-all-start) | async-done | bytes 786464 | tf_op jit(solution)/shard_map/all_to_all | solution.py:57
  47.7 30.6 %all_gather.50 = bf16[768,384]{1,0:T(8,128)(2,1)} all-gather(bf16[48,384]{1,0:T(8,128)(2,1)S(1)} %copy-done.62), channel_id=1, replica_groups=mesh['dp'=16,'tensor'=2] {'dp'}, dimensions={0}, use_global_device_ids=true | all-gather | bytes 626688 | tf_op jit(solution)/shard_map/all_gather | solution.py:115
  78.4 23.1 %all_gather.51 = bf16[768,384]{1,0:T(8,128)(2,1)} all-gather(bf16[48,384]{1,0:T(8,128)(2,1)S(1)} %copy-done.63), channel_id=1, replica_groups=mesh['dp'=16,'tensor'=2] {'dp'}, dimensions={0}, use_global_device_ids=true | all-gather | bytes 626688 | tf_op jit(solution)/shard_map/all_gather | solution.py:116
  101.5 19.0 %all_gather.49 = bf16[768,384]{1,0:T(8,128)(2,1)S(1)} all-gather(bf16[48,384]{1,0:T(8,128)(2,1)S(1)} %copy-done.64), channel_id=1, replica_groups=mesh['dp'=16,'tensor'=2] {'dp'}, dimensions={0}, use_global_device_ids=true | all-gather | bytes 626688 | tf_op jit(solution)/shard_map/all_gather | solution.py:117
  120.5 21.8 %all_gather.52 = bf16[768,384]{1,0:T(8,128)(2,1)} all-gather(bf16[48,384]{1,0:T(8,128)(2,1)S(1)} %copy-done.65), channel_id=1, replica_groups=mesh['dp'=16,'tensor'=2] {'dp'}, dimensions={0}, use_global_device_ids=true | all-gather | bytes 626688 | tf_op jit(solution)/shard_map/all_gather | solution.py:118
  146.1 12.2 %all_gather.56 = bf16[512,768]{1,0:T(8,128)(2,1)S(1)} all-gather(bf16[256,768]{1,0:T(8,128)(2,1)S(1)} %squeeze.36), channel_id=1, replica_groups=mesh['dp'=16,'tensor'=2] {'tensor'}, dimensions={0}, use_global_device_ids=true | all-gather | bytes 1179648 | tf_op jit(solution)/shard_map/all_gather | solution.py:127
  158.3 11.7 %all_gather.48 = bf16[512,768]{1,0:T(8,128)(2,1)S(1)} all-gather(bf16[256,768]{1,0:T(8,128)(2,1)S(1)} %squeeze.34), channel_id=1, replica_groups=mesh['dp'=16,'tensor'=2] {'tensor'}, dimensions={0}, use_global_device_ids=true | all-gather | bytes 1179648 | tf_op jit(solution)/shard_map/all_gather | solution.py:127
  199.4 19.1 %reduce-scatter.19.cloned.1.call-done = bf16[256,768]{1,0:T(8,128)(2,1)} async-done(((bf16[512,768]{1,0:T(8,128)(2,1)}), bf16[256,768]{1,0:T(8,128)(2,1)}) %reduce-scatter.19.cloned.1.call-update) | async-done | bytes 393232 | tf_op jit(solution)/shard_map/reduce_scatter | solution.py:160
  223.4 11.7 %all_gather.57 = bf16[512,768]{1,0:T(8,128)(2,1)} all-gather(bf16[256,768]{1,0:T(8,128)(2,1)S(1)} %get-tuple-element.81), channel_id=1, replica_groups=mesh['dp'=16,'tensor'=2] {'tensor'}, dimensions={0}, use_global_device_ids=true | all-gather | bytes 1179648 | tf_op jit(solution)/shard_map/all_gather | solution.py:171
  240.6 37.8 %all-gather.5.cloned.1.call-done = bf16[768,1536]{1,0:T(8,128)(2,1)} async-done(((bf16[48,1536]{1,0:T(8,128)(2,1)}), bf16[768,1536]{1,0:T(8,128)(2,1)}) %all-gather.5.cloned.1.call-update) | async-done | bytes 2359312 | tf_op jit(solution)/shard_map/all_gather | solution.py:120
  282.9 18.1 %all_gather.53 = bf16[512,768]{1,0:T(8,128)(2,1)S(1)} all-gather(bf16[256,768]{1,0:T(8,128)(2,1)S(1)} %get-tuple-element.80), channel_id=1, replica_groups=mesh['dp'=16,'tensor'=2] {'tensor'}, dimensions={0}, use_global_device_ids=true | all-gather | bytes 1179648 | tf_op jit(solution)/shard_map/all_gather | solution.py:171
  311.4 13.9 %reduce-scatter.17.cloned.1.call-done = bf16[256,768]{1,0:T(8,128)(2,1)} async-done(((bf16[512,768]{1,0:T(8,128)(2,1)}), bf16[256,768]{1,0:T(8,128)(2,1)}) %reduce-scatter.17.cloned.1.call-update) | async-done | bytes 393232 | tf_op jit(solution)/shard_map/reduce_scatter | solution.py:175
  351.3 15.6 %all_gather.60 = bf16[512,768]{1,0:T(8,128)(2,1)S(1)} all-gather(bf16[256,768]{1,0:T(8,128)(2,1)} %get-tuple-element.76), channel_id=1, replica_groups=mesh['dp'=16,'tensor'=2] {'tensor'}, dimensions={0}, use_global_device_ids=true | all-gather | bytes 1179648 | tf_op jit(solution)/shard_map/all_gather | solution.py:192
  378.4 14.6 %reduce-scatter.27.cloned.1.call-done = bf16[256,768]{1,0:T(8,128)(2,1)} async-done(((bf16[512,768]{1,0:T(8,128)(2,1)}), bf16[256,768]{1,0:T(8,128)(2,1)}) %reduce-scatter.27.cloned.1.call-update) | async-done | bytes 393232 | tf_op jit(solution)/shard_map/reduce_scatter | solution.py:196
  427.7 12.1 %convert_reduce_fusion.8 = (f32[6,64]{1,0:T(8,128)S(1)}, bf16[6,64,512]{2,1,0:T(8,128)(2,1)}) fusion(bf16[512,6,64]{0,2,1:T(8,128)(2,1)S(1)} %bitcast.190, f32[6,512,512]{1,2,0:T(8,128)} %fusion.131, f32[6,512,512]{1,2,0:T(8,128)} %copy-done.3, f32[6,512]{1,0:T(8,128)S(1)} %copy-done.60), kind=kOutput, calls=%fused_computation.132 | convolution fusion | flops 212929664 | bytes 13383168 | tf_op jit(solution)/shard_map/hqk,khd->qhd/dot_general | solution.py:231
  461.4 12.4 %fusion.63 = bf16[6,64,512]{2,1,0:T(8,128)(2,1)} fusion(bf16[512,6,64]{0,2,1:T(8,128)(2,1)} %bitcast.188, f32[6,512,512]{1,2,0:T(8,128)} %fusion.128, f32[6,512,512]{1,2,0:T(8,128)} %copy-done.2, f32[6,512]{1,0:T(8,128)} %log_add_fusion.1), kind=kOutput, calls=%fused_computation.85 | convolution fusion | flops 212536832 | bytes 13381632 | tf_op jit(solution)/shard_map/hqk,qhd->khd/dot_general | solution.py:235
  473.7 12.8 %convert_reduce_fusion.9 = (f32[6,64]{1,0:T(8,128)}, bf16[6,64,512]{2,1,0:T(8,128)(2,1)}) fusion(bf16[512,6,64]{0,2,1:T(8,128)(2,1)} %bitcast.186, f32[6,512,512]{1,2,0:T(8,128)} %fusion.128, f32[6,512,512]{1,2,0:T(8,128)} %copy-done.2, f32[6,512]{1,0:T(8,128)} %log_add_fusion.1), kind=kOutput, calls=%fused_computation.133 | convolution fusion | flops 212929664 | bytes 13383168 | tf_op jit(solution)/shard_map/hqk,khd->qhd/dot_general | solution.py:231
  535.0 19.8 %all-to-all-done.2 = bf16[2,16,12288]{2,0,1:T(2,128)(2,1)S(1)} async-done(((bf16[2,16,12288]{2,0,1:T(2,128)(2,1)}), bf16[2,16,12288]{2,0,1:T(2,128)(2,1)S(1)}, u32[]{:S(2)}, u32[]{:S(2)}) %all-to-all-start.2) | async-done | bytes 786464 | tf_op jit(solution)/shard_map/all_to_all | solution.py:57
  567.5 40.7 %all-reduce = (f32[2,768]{1,0:T(2,128)S(1)}, f32[6,768]{1,0:T(8,128)S(1)}, f32[3072]{0:T(1024)S(1)}) all-reduce(f32[2,768]{1,0:T(2,128)S(1)} %pad_maximum_fusion.2, f32[6,768]{1,0:T(8,128)S(1)} %add.376, f32[3072]{0:T(1024)S(1)} %mul.447), channel_id=1, replica_groups=mesh['dp'=16,'tensor'=2] {'dp','tensor'}, use_global_device_ids=true, to_apply=%region_41.43 | all-reduce | flops 9216 | bytes 73728 | tf_op jit(solution)/shard_map/psum | solution.py:294
  612.4 28.3 %reduce-scatter.35.cloned.1.call-done = f32[48,384]{1,0:T(8,128)} async-done(((f32[768,384]{1,0:T(8,128)}), f32[48,384]{1,0:T(8,128)}) %reduce-scatter.35.cloned.1.call-update) | async-done | bytes 73744 | tf_op jit(solution)/shard_map/reduce_scatter | solution.py:284
  640.7 61.2 %reduce-scatter.31.cloned.1.call-done = f32[48,384]{1,0:T(8,128)} async-done(((f32[768,384]{1,0:T(8,128)}), f32[48,384]{1,0:T(8,128)}) %reduce-scatter.31.cloned.1.call-update) | async-done | bytes 73744 | tf_op jit(solution)/shard_map/reduce_scatter | solution.py:282
  701.9 61.1 %reduce-scatter.33.cloned.1.call-done = f32[48,384]{1,0:T(8,128)} async-done(((f32[768,384]{1,0:T(8,128)}), f32[48,384]{1,0:T(8,128)}) %reduce-scatter.33.cloned.1.call-update) | async-done | bytes 73744 | tf_op jit(solution)/shard_map/reduce_scatter | solution.py:283
  763.0 79.0 %reduce-scatter.39.cloned.1.call-done = f32[48,1536]{1,0:T(8,128)} async-done(((f32[768,1536]{1,0:T(8,128)}), f32[48,1536]{1,0:T(8,128)}) %reduce-scatter.39.cloned.1.call-update) | async-done | bytes 294928 | tf_op jit(solution)/shard_map/reduce_scatter | solution.py:286
  842.0 79.4 %reduce-scatter.41.cloned.1.call-done = f32[48,1536]{1,0:T(8,128)} async-done(((f32[768,1536]{1,0:T(8,128)}), f32[48,1536]{1,0:T(8,128)}) %reduce-scatter.41.cloned.1.call-update) | async-done | bytes 294928 | tf_op jit(solution)/shard_map/reduce_scatter | solution.py:287
  (383 shorter events, 238.4 us)
Async XLA Ops:
  11.2 26.1 %all-to-all-start = ((bf16[2,16,12288]{2,0,1:T(2,128)(2,1)}), bf16[2,16,12288]{2,0,1:T(2,128)(2,1)S(1)}, u32[]{:S(2)}, u32[]{:S(2)}) async-start(bf16[2,16,12288]{2,0,1:T(2,128)(2,1)} %copy.72), calls=%async_computation | async-start | bytes 1572864 | tf_op jit(solution)/shard_map/all_to_all | solution.py:57
  38.7 62.8 %copy-start.64 = (bf16[48,384]{1,0:T(8,128)(2,1)S(1)}, bf16[48,384]{1,0:T(8,128)(2,1)}, u32[]{:S(2)}) copy-start(bf16[48,384]{1,0:T(8,128)(2,1)} %param.27) | copy-start | bytes 110596
  38.7 81.8 %copy-start.65 = (bf16[48,384]{1,0:T(8,128)(2,1)S(1)}, bf16[48,384]{1,0:T(8,128)(2,1)}, u32[]{:S(2)}) copy-start(bf16[48,384]{1,0:T(8,128)(2,1)} %param.28) | copy-start | bytes 110596
  40.2 102.1 %all-to-all-start.1 = ((bf16[16,2,12288]{2,1,0:T(2,128)(2,1)}), bf16[16,2,12288]{2,1,0:T(2,128)(2,1)S(1)}, u32[]{:S(2)}, u32[]{:S(2)}) async-start(bf16[16,2,12288]{2,1,0:T(2,128)(2,1)} %all_to_all.54), calls=%async_computation.1 | async-start | bytes 1572864 | tf_op jit(solution)/shard_map/all_to_all | solution.py:59
  45.7 152.4 %reduce-scatter.15.cloned.1.call-start = ((), (), s32[]{:S(2)}) async-start(), calls=%async_computation.18 | async-start | bytes 1179648 | tf_op jit(solution)/shard_map/reduce_scatter | solution.py:160
  120.5 65.4 %copy-start.8 = (bf16[768,384]{1,0:T(8,128)(2,1)}, bf16[768,384]{1,0:T(8,128)(2,1)S(1)}, u32[]{:S(2)}) copy-start(bf16[768,384]{1,0:T(8,128)(2,1)S(1)} %all_gather.49) | copy-start | bytes 1769476
  183.3 35.3 %reduce-scatter.19.cloned.1.call-start = ((), (), s32[]{:S(2)}) async-start(), calls=%async_computation.22 | async-start | bytes 1179648 | tf_op jit(solution)/shard_map/reduce_scatter | solution.py:160
  192.2 42.9 %all-gather.3.cloned.1.call-start = ((), (), s32[]{:S(2)}) async-start(), calls=%async_computation.19 | async-start | bytes 2506752 | tf_op jit(solution)/shard_map/all_gather | solution.py:119
  192.8 85.6 %all-gather.5.cloned.1.call-start = ((), (), s32[]{:S(2)}) async-start(), calls=%async_computation.20 | async-start | bytes 2506752 | tf_op jit(solution)/shard_map/all_gather | solution.py:120
  193.4 118.0 %reduce-scatter.21.cloned.1.call-start = ((), (), s32[]{:S(2)}) async-start(), calls=%async_computation.23 | async-start | bytes 1179648 | tf_op jit(solution)/shard_map/reduce_scatter | solution.py:175
  282.9 42.3 %reduce-scatter.17.cloned.1.call-start = ((), (), s32[]{:S(2)}) async-start(), calls=%async_computation.21 | async-start | bytes 1179648 | tf_op jit(solution)/shard_map/reduce_scatter | solution.py:175
  309.4 69.0 %reduce-scatter.23.cloned.1.call-start = ((), (), s32[]{:S(2)}) async-start(), calls=%async_computation.24 | async-start | bytes 1179648 | tf_op jit(solution)/shard_map/reduce_scatter | solution.py:196
  351.2 41.8 %reduce-scatter.27.cloned.1.call-start = ((), (), s32[]{:S(2)}) async-start(), calls=%async_computation.26 | async-start | bytes 1179648 | tf_op jit(solution)/shard_map/reduce_scatter | solution.py:196
  375.5 146.7 %reduce-scatter.29.cloned.1.call-start = ((), (), s32[]{:S(2)}) async-start(), calls=%async_computation.27 | async-start | bytes 1179648 | tf_op jit(solution)/shard_map/reduce_scatter | solution.py:254
  456.1 68.3 %reduce-scatter.25.cloned.1.call-start = ((), (), s32[]{:S(2)}) async-start(), calls=%async_computation.25 | async-start | bytes 1179648 | tf_op jit(solution)/shard_map/reduce_scatter | solution.py:254
  495.5 116.9 %reduce-scatter.37.cloned.1.call-start = ((), (), s32[]{:S(2)}) async-start(), calls=%async_computation.31 | async-start | bytes 1253376 | tf_op jit(solution)/shard_map/reduce_scatter | solution.py:285
  500.3 140.4 %reduce-scatter.35.cloned.1.call-start = ((), (), s32[]{:S(2)}) async-start(), calls=%async_computation.30 | async-start | bytes 1253376 | tf_op jit(solution)/shard_map/reduce_scatter | solution.py:284
  502.6 199.3 %reduce-scatter.31.cloned.1.call-start = ((), (), s32[]{:S(2)}) async-start(), calls=%async_computation.28 | async-start | bytes 1253376 | tf_op jit(solution)/shard_map/reduce_scatter | solution.py:282
  505.3 257.8 %reduce-scatter.33.cloned.1.call-start = ((), (), s32[]{:S(2)}) async-start(), calls=%async_computation.29 | async-start | bytes 1253376 | tf_op jit(solution)/shard_map/reduce_scatter | solution.py:283
  507.7 334.4 %reduce-scatter.39.cloned.1.call-start = ((), (), s32[]{:S(2)}) async-start(), calls=%async_computation.32 | async-start | bytes 5013504 | tf_op jit(solution)/shard_map/reduce_scatter | solution.py:286
  514.4 407.0 %reduce-scatter.41.cloned.1.call-start = ((), (), s32[]{:S(2)}) async-start(), calls=%async_computation.33 | async-start | bytes 5013504 | tf_op jit(solution)/shard_map/reduce_scatter | solution.py:287
  528.5 26.3 %all-to-all-start.2 = ((bf16[2,16,12288]{2,0,1:T(2,128)(2,1)}), bf16[2,16,12288]{2,0,1:T(2,128)(2,1)S(1)}, u32[]{:S(2)}, u32[]{:S(2)}) async-start(bf16[2,16,12288]{2,0,1:T(2,128)(2,1)} %pad_maximum_fusion.1), calls=%async_computation.10 | async-start | bytes 1572864 | tf_op jit(solution)/shard_map/all_to_all | solution.py:57
  556.5 365.0 %copy-start.1 = (s32[32]{0:T(128)S(1)}, s32[32]{0:T(128)}, u32[]{:S(2)}) copy-start(s32[32]{0:T(128)} %param.23) | copy-start | bytes 388
  557.9 52.9 %all-to-all-start.3 = ((bf16[16,2,12288]{2,1,0:T(2,128)(2,1)}), bf16[16,2,12288]{2,1,0:T(2,128)(2,1)S(1)}, u32[]{:S(2)}, u32[]{:S(2)}) async-start(bf16[16,2,12288]{2,1,0:T(2,128)(2,1)} %all_to_all.60), calls=%async_computation.11 | async-start | bytes 1572864 | tf_op jit(solution)/shard_map/all_to_all | solution.py:59
  (92 other events, 689.9 us)
Sparse Core Ops, SparseCore 0:
  183.4 14.6 reduce-scatter.14
  201.0 17.4 reduce-scatter.18
  283.0 21.3 reduce-scatter.20
  309.6 15.6 reduce-scatter.16
  351.3 20.2 reduce-scatter.22
  375.6 17.4 reduce-scatter.26
  456.2 17.3 reduce-scatter.28
  495.7 17.4 reduce-scatter.24
  517.4 61.8 reduce-scatter.36
  583.3 57.3 reduce-scatter.34
  644.9 56.9 reduce-scatter.30
  705.9 57.0 reduce-scatter.32
  767.5 74.5 reduce-scatter.38
  846.8 74.5 reduce-scatter.40
Sparse Core Ops, SparseCore 1:
  195.0 40.0 all-gather.2
  237.2 41.2 all-gather.4
where the time goes:
time: 936 us; the launch traced here: 929 us
  waiting for transfers between devices  437 us (47%)
  blocking collectives  238 us (25%)
  matrix products  143 us (15%)
  other arithmetic  34.4 us (4%)
  local copies, waits for them, and re-layouts  30.8 us (3%)
  starting transfers between devices  28.1 us (3%)
  between operations  17 us (2%)
    reduce_scatter x1, waiting for transfers between devices, on_device(): lax.psum_scatter(acc_down, 'dp', scatter_dimension=0, tiled=True)  79.4 us
    reduce_scatter x1, waiting for transfers between devices, on_device(): lax.psum_scatter(acc_up, 'dp', scatter_dimension=0, tiled=True)  79 us
    reduce_scatter x1, waiting for transfers between devices, on_device(): lax.psum_scatter(acc_query, 'dp', scatter_dimension=0, tiled=True)  61.2 us
    reduce_scatter x1, waiting for transfers between devices, on_device(): lax.psum_scatter(acc_key, 'dp', scatter_dimension=0, tiled=True)  61.1 us
    psum x1, blocking collectives, on_device(): lax.psum((sum_vectors, jnp.stack([place_part(sum_qbias), place_part(sum_v...  40.7 us
    all_gather x1, waiting for transfers between devices, on_device(): lax.all_gather(down_weight, 'dp', axis=0, tiled=True)  37.8 us
    all_to_all x2, waiting for transfers between devices, deal_rows(): lax.all_to_all(flattened, 'dp', split_axis=1, concat_axis=0, tiled=True)  37.1 us
    all_gather x1, blocking collectives, on_device(): lax.all_gather(query_weight, 'dp', axis=0, tiled=True)  30.6 us
  transfers between devices with their start and end apart: 20, of which 12 were waited for; matrix products, arithmetic and copies ran while one was open for 12% of the time, Pallas kernels for 0%

commit v1 on v0

v1 whole, which is shorter than its diff:
```python
import jax
import jax.numpy as jnp
from jax import lax
from jax.experimental import pallas as pl
from jax.experimental.pallas import tpu as pltpu
from jax.sharding import PartitionSpec as P

HEAD = 64
EPSILON = 1e-05
SQRT_HALF = 0.7071067811865476
INV_ROOT_TWO_PI = 0.3989422804014327
BOTH = ("dp", "tensor")
F32 = jnp.float32
BF16 = jnp.bfloat16


def norm_forward(inputs, gain, offset):
    center = inputs - jnp.mean(inputs, axis=-1, keepdims=True)
    rscale = lax.rsqrt(jnp.mean(center * center, axis=-1, keepdims=True) + EPSILON)
    normal = center * rscale
    return normal * gain + offset, normal, rscale


def norm_backward(incoming, normal, rscale, gain):
    scaled = incoming * gain
    inner = (
        scaled
        - jnp.mean(scaled, axis=-1, keepdims=True)
        - normal * jnp.mean(scaled * normal, axis=-1, keepdims=True)
    )
    return rscale * inner, jnp.sum(incoming * normal, axis=0), jnp.sum(incoming, axis=0)


def gelu(v):
    return 0.5 * v * (1.0 + lax.erf(v * SQRT_HALF))


def gelu_slope(v):
    return 0.5 * (1.0 + lax.erf(v * SQRT_HALF)) + v * jnp.exp(-0.5 * v * v) * INV_ROOT_TWO_PI


def dot_nn(a, b):
    return jnp.dot(a, b, preferred_element_type=F32)


def dot_tn(a, b):
    return lax.dot_general(a, b, (((0,), (0,)), ((), ())), preferred_element_type=F32)


def dot_nt(a, b):
    return lax.dot_general(a, b, (((1,), (1,)), ((), ())), preferred_element_type=F32)


def gather_weight(shard):
    tensor_size = lax.axis_size("tensor")
    rows, cols = shard.shape
    got = lax.all_gather(shard, BOTH, axis=0, tiled=False)
    got = got.reshape(-1, tensor_size, rows, cols)
    return got.transpose(0, 2, 1, 3).reshape(-1, tensor_size * cols)


def scatter_grad(grad, rows, cols):
    tensor_size = lax.axis_size("tensor")
    parts = grad.reshape(-1, rows, tensor_size, cols).transpose(0, 2, 1, 3)
    parts = parts.reshape(-1, cols).astype(BF16)
    return lax.psum_scatter(parts, BOTH, scatter_dimension=0, tiled=True).astype(F32)


def pick_kernel(order, src, dst, sems):
    def copy(t):
        return pltpu.make_async_copy(src.at[order[t]], dst.at[t], sems.at[t])

    count = dst.shape[0]
    for t in range(count):
        copy(t).start()
    for t in range(count):
        copy(t).wait()


def pick(pieces, order):
    return pl.pallas_call(
        pick_kernel,
        out_shape=jax.ShapeDtypeStruct(pieces.shape, pieces.dtype),
        in_specs=[pl.BlockSpec(memory_space=pltpu.SMEM), pl.BlockSpec(memory_space=pl.ANY)],
        out_specs=pl.BlockSpec(memory_space=pl.ANY),
        scratch_shapes=[pltpu.SemaphoreType.DMA((pieces.shape[0],))],
        name="pick",
    )(order, pieces)


def slots_to_initial(block, inverse):
    micro, half, features = block.shape
    dp, tensor_size = lax.axis_size("dp"), lax.axis_size("tensor")
    piece = half // dp
    spread = lax.all_to_all(
        block.reshape(micro, dp, piece, features), "dp", split_axis=1, concat_axis=0, tiled=True
    ).reshape(micro * dp, piece, features)
    chosen = pick(spread, inverse)
    got = lax.all_to_all(chosen, BOTH, split_axis=0, concat_axis=0, tiled=True)
    return got.reshape(dp, tensor_size, piece, features).transpose(1, 0, 2, 3).reshape(-1, features)


def initial_to_slots(rows, slot_order, micro):
    dp, tensor_size = lax.axis_size("dp"), lax.axis_size("tensor")
    features = rows.shape[-1]
    piece = rows.shape[0] // (dp * tensor_size)
    pieces = rows.reshape(tensor_size, dp, piece, features).transpose(1, 0, 2, 3)
    got = lax.all_to_all(
        pieces.reshape(-1, piece, features), BOTH, split_axis=0, concat_axis=0, tiled=True
    )
    chosen = pick(got, slot_order)
    back = lax.all_to_all(chosen, "dp", split_axis=0, concat_axis=0, tiled=True)
    back = back.reshape(dp, micro, piece, features).transpose(1, 0, 2, 3)
    return back.reshape(micro, dp * piece, features)


def on_device(
    tokens, cotangent, lengths, slot_order,
    query_weight, key_weight, value_weight, out_weight, up_weight, down_weight,
    query_bias, value_bias, out_bias, up_bias, down_bias,
    first_gain, first_offset, second_gain, second_offset,
):
    micro, half, features = tokens.shape
    dp, tensor_size = lax.axis_size("dp"), lax.axis_size("tensor")
    dp_pos, tensor_pos = lax.axis_index("dp"), lax.axis_index("tensor")
    seq_len = half * tensor_size
    heads = features // HEAD
    slot_count = slot_order.shape[0]
    inverse = jnp.zeros_like(slot_order).at[slot_order].set(jnp.arange(slot_count, dtype=jnp.int32))
    live_len = lengths[dp_pos * tensor_size + tensor_pos]
    positions = jnp.arange(seq_len, dtype=jnp.int32)
    live = positions < live_len
    live_col = live.astype(F32)[:, None]

    x = lax.all_to_all(tokens, "tensor", split_axis=0, concat_axis=1, tiled=True)[0]
    wq, wk, wv, wo, wu, wd = (
        gather_weight(w)
        for w in (query_weight, key_weight, value_weight, out_weight, up_weight, down_weight)
    )
    bq = lax.all_gather(query_bias, "tensor", axis=0, tiled=True)
    bv = lax.all_gather(value_bias, "tensor", axis=0, tiled=True)
    bu = lax.all_gather(up_bias, "tensor", axis=0, tiled=True)
    cot = slots_to_initial(cotangent, inverse)

    split = (seq_len, heads, HEAD)
    scale = HEAD**-0.5
    q = (dot_nn(x, wq) + bq).astype(BF16).reshape(split)
    k = dot_nn(x, wk).astype(BF16).reshape(split)
    v = (dot_nn(x, wv) + bv).astype(BF16).reshape(split)
    s = jnp.einsum("qhd,khd->hqk", q, k, preferred_element_type=F32) * scale
    s = jnp.where(live[None, None, :], s, -1e9)
    row_max = jnp.max(s, axis=-1, keepdims=True)
    raised = jnp.exp(s - row_max)
    total = jnp.sum(raised, axis=-1, keepdims=True)
    probs = raised / total
    probs_low = probs.astype(BF16)
    attended = jnp.einsum("hqk,khd->qhd", probs_low, v, preferred_element_type=F32)
    attended = attended.astype(BF16).reshape(seq_len, features)
    attn_out = dot_nt(attended, wo) + out_bias
    normed, n1, r1 = norm_forward(x.astype(F32) + attn_out, first_gain, first_offset)
    normed_low = normed.astype(BF16)
    hidden = dot_nn(normed_low, wu) + bu
    act = gelu(hidden).astype(BF16)
    ffn_out = dot_nt(act, wd) + down_bias
    final, n2, r2 = norm_forward(normed + ffn_out, second_gain, second_offset)
    layer_out = initial_to_slots((final * live_col).astype(BF16), slot_order, micro)

    grad_out = cot.astype(F32) * live_col
    grad_second, gain_two, offset_two = norm_backward(grad_out, n2, r2, second_gain)
    gffn = grad_second.astype(BF16)
    grad_act = dot_nn(gffn, wd)
    ghid = (grad_act * gelu_slope(hidden)).astype(BF16)
    grad_normed = dot_nt(ghid, wu) + grad_second
    d_down = dot_tn(gffn, act)
    d_up = dot_tn(normed_low, ghid)
    grad_first, gain_one, offset_one = norm_backward(grad_normed, n1, r1, first_gain)
    gattn = grad_first.astype(BF16)
    gatt = dot_nn(gattn, wo).astype(BF16)
    d_out = dot_tn(gattn, attended)
    gatt_h = gatt.reshape(split)
    gp = jnp.einsum("qhd,khd->hqk", gatt_h, v, preferred_element_type=F32)
    inner = jnp.sum(gp * probs, axis=-1, keepdims=True)
    gs = (probs * (gp - inner) * scale).astype(BF16)
    gq = jnp.einsum("hqk,khd->qhd", gs, k, preferred_element_type=F32)
    gk = jnp.einsum("hqk,qhd->khd", gs, q, preferred_element_type=F32)
    gv = jnp.einsum("hqk,qhd->khd", probs_low, gatt_h, preferred_element_type=F32)
    gq, gk, gv = (g.astype(BF16).reshape(seq_len, features) for g in (gq, gk, gv))
    grad_tokens = (grad_first + dot_nt(gq, wq) + dot_nt(gk, wk) + dot_nt(gv, wv)).astype(BF16)
    input_grad = lax.all_to_all(
        grad_tokens.reshape(1, seq_len, features), "tensor", split_axis=1, concat_axis=0, tiled=True
    )
    rows, cols = query_weight.shape
    units = up_weight.shape[1]
    grads = (
        scatter_grad(dot_tn(x, gq), rows, cols),
        scatter_grad(dot_tn(x, gk), rows, cols),
        scatter_grad(dot_tn(x, gv), rows, cols),
        scatter_grad(d_out, rows, cols),
        scatter_grad(d_up, rows, units),
        scatter_grad(d_down, rows, units),
    )

    def colsum(a):
        return jnp.sum(a.astype(F32), axis=0)

    sums = lax.psum(
        jnp.concatenate([
            colsum(gq), colsum(gv), colsum(gattn), colsum(ghid), colsum(gffn),
            gain_one, offset_one, gain_two, offset_two,
        ]),
        BOTH,
    )
    pieces = []
    at = 0
    for width in (features, features, features, units * tensor_size, *(features,) * 5):
        pieces.append(sums[at : at + width])
        at += width

    def own(vec, width):
        return lax.dynamic_slice_in_dim(vec, tensor_pos * width, width)

    return (
        layer_out, input_grad, *grads,
        own(pieces[0], cols), own(pieces[1], cols), pieces[2], own(pieces[3], units), *pieces[4:],
    )


def solution(mesh):
    rows = P("dp", "tensor", None)
    weight = P("dp", "tensor")
    cut = P("tensor")
    whole = P()
    return jax.shard_map(
        on_device,
        mesh=mesh,
        in_specs=(rows, rows, whole, whole, *(weight,) * 6, cut, cut, whole, cut, *(whole,) * 5),
        out_specs=(rows, rows, *(weight,) * 6, cut, cut, whole, cut, *(whole,) * 5),
        check_vma=False,
    )
```

time: 936 us -> 1050 us (1.12)
  waiting for transfers between devices: 437 us -> 594 us
  blocking collectives: 238 us -> 91.5 us
  local copies, waits for them, and re-layouts: 30.8 us -> 131 us
  Pallas kernels: 0 us -> 51.8 us
  matrix products: 143 us -> 119 us
  other arithmetic: 34.4 us -> 22.4 us
    all_gather x12 -> x3, blocking collectives: 198 us -> 20.8 us  [the longest x1 12 us: on_device(): bq = lax.all_gather(query_bias, 'tensor', axis=0, tiled=True)]
    all_gather x2 -> x6, waiting for transfers between devices: 37.8 us -> 212 us  [gather_weight(): got = lax.all_gather(shard, BOTH, axis=0, tiled=False)]
    convert_element_type x0 -> x18, local copies, waits for them, and re-layouts: none -> 67.5 us  [the longest x13 59.6 us: scatter_grad(): parts = parts.reshape(-1, cols).astype(BF16)]
    pallas_call x0 -> x2, Pallas kernels: none -> 51.8 us  [pick(): pl.pallas_call(pick_kernel, out_shape=jax.ShapeDtypeStruct(pieces.shape,...]
    dot_general x48 -> x23, matrix products: 143 us -> 111 us  [the longest x6 24.3 us: dot_tn(): lax.dot_general(a, b, (((0,), (0,)), ((), ())), preferred_element_type=F32)]
    reshape x1 -> x9, local copies, waits for them, and re-layouts: 1.24 us -> 31.2 us  [the longest x6 27.8 us: gather_weight(): got = got.reshape(-1, tensor_size, rows, cols)]
    all_to_all x0 -> x1, blocking collectives: none -> 28.5 us  [slots_to_initial(): lax.all_to_all(block.reshape(micro, dp, piece, features), 'dp', split_axi...]
    all_to_all x4 -> x5, waiting for transfers between devices: 37.1 us -> 10.9 us  [the longest x1 10.9 us: initial_to_slots(): lax.all_to_all(pieces.reshape(-1, piece, features), BOTH, split_axis=0, c...]
  transfers between devices with their start and end apart: 20 -> 17, of which waited for: 12 -> 10; matrix products, arithmetic and copies ran while one was open for 12% -> 21% of each run, Pallas kernels for 0% -> 5%
where the time goes in v1:
time: 1050 us; the launch traced here: 1040 us
  waiting for transfers between devices  594 us (57%)
  local copies, waits for them, and re-layouts  131 us (12%)
  matrix products  119 us (11%)
  blocking collectives  91.5 us (9%)
  Pallas kernels  51.8 us (5%)
  other arithmetic  22.4 us (2%)
  starting transfers between devices  18.4 us (2%)
  between operations  15.2 us (1%)
    reduce_scatter x6, waiting for transfers between devices, scatter_grad(): lax.psum_scatter(parts, BOTH, scatter_dimension=0, tiled=True).astype(F32)  367 us
    all_gather x6, waiting for transfers between devices, gather_weight(): got = lax.all_gather(shard, BOTH, axis=0, tiled=False)  212 us
    convert_element_type x13, local copies, waits for them, and re-layouts, scatter_grad(): parts = parts.reshape(-1, cols).astype(BF16)  59.6 us
    pallas_call x2, Pallas kernels, pick(): pl.pallas_call(pick_kernel, out_shape=jax.ShapeDtypeStruct(pieces.shape,...  51.8 us
    psum x1, blocking collectives, on_device(): lax.psum(jnp.concatenate([colsum(gq), colsum(gv), colsum(gattn), colsum(g...  42.3 us
    all_to_all x1, blocking collectives, slots_to_initial(): lax.all_to_all(block.reshape(micro, dp, piece, features), 'dp', split_axi...  28.5 us
    reshape x6, local copies, waits for them, and re-layouts, gather_weight(): got = got.reshape(-1, tensor_size, rows, cols)  27.8 us
    unnamed x107, local copies, waits for them, and re-layouts  24.3 us
  transfers between devices with their start and end apart: 17, of which 10 were waited for; matrix products, arithmetic and copies ran while one was open for 21% of the time, Pallas kernels for 5%

profile of v1, /device:TPU:0, one launch (start us, length us, event | category | flops | bytes accessed | tf_op | source)
XLA Modules:
  0.0 1043.1 jit_solution(13643160840422524582)
XLA Ops:
  12.4 28.5 %all_to_all.51 = bf16[2,16,16,768]{3,2,0,1:T(8,128)(2,1)} all-to-all(bf16[2,16,16,768]{3,2,0,1:T(8,128)(2,1)S(1)} %copy.178), channel_id=1, replica_groups=mesh['dp'=16,'tensor'=2] {'dp'}, dimensions={1} | all-to-all | bytes 1572864 | tf_op jit(solution)/shard_map/all_to_all | solution.py:95
  44.5 12.0 %all-gather.7 = f32[2,1,384]{2,1,0:T(1,128)S(1)} all-gather(f32[1,1,384]{2,1,0:T(1,128)S(1)} %reshape.293), channel_id=1, replica_groups=mesh['dp'=16,'tensor'=2] {'tensor'}, dimensions={0}, use_global_device_ids=true | all-gather | bytes 4608 | tf_op jit(solution)/shard_map/all_gather | solution.py:140
  70.8 25.9 %pick.3 = bf16[32,16,768]{2,1,0:T(8,128)(2,1)} custom-call(s32[32]{0:T(128)} %scatter_custom_fusion.order, bf16[32,16,768]{2,1,0:T(8,128)(2,1)} %bitcast.198), custom_call_target="tpu_custom_call" | custom-call | tf_op jit(solution)/shard_map/pick/pallas_call | solution.py:81
  99.1 26.1 %all-gather.20.cloned.1.call-done = bf16[1536,384]{1,0:T(8,128)(2,1)} async-done(((bf16[48,384]{1,0:T(8,128)(2,1)}), bf16[1536,384]{1,0:T(8,128)(2,1)}) %all-gather.20.cloned.1.call-update) | async-done | bytes 1179664 | tf_op jit(solution)/shard_map/all_gather | solution.py:57
  128.7 52.6 %all-gather.16.cloned.1.call-done = bf16[1536,384]{1,0:T(8,128)(2,1)} async-done(((bf16[48,384]{1,0:T(8,128)(2,1)}), bf16[1536,384]{1,0:T(8,128)(2,1)}) %all-gather.16.cloned.1.call-update) | async-done | bytes 1179664 | tf_op jit(solution)/shard_map/all_gather | solution.py:57
  199.9 7.6 fusion.61
  214.3 24.5 %all-gather.22.cloned.1.call-done = bf16[1536,384]{1,0:T(8,128)(2,1)} async-done(((bf16[48,384]{1,0:T(8,128)(2,1)}), bf16[1536,384]{1,0:T(8,128)(2,1)}) %all-gather.22.cloned.1.call-update) | async-done | bytes 1179664 | tf_op jit(solution)/shard_map/all_gather | solution.py:57
  245.2 58.9 %all-gather.24.cloned.1.call-done = bf16[1536,1536]{1,0:T(8,128)(2,1)} async-done(((bf16[48,1536]{1,0:T(8,128)(2,1)}), bf16[1536,1536]{1,0:T(8,128)(2,1)}) %all-gather.24.cloned.1.call-update) | async-done | bytes 4718608 | tf_op jit(solution)/shard_map/all_gather | solution.py:57
  304.2 9.4 copy.174
  319.3 50.1 %all-gather.26.cloned.1.call-done = bf16[1536,1536]{1,0:T(8,128)(2,1)} async-done(((bf16[48,1536]{1,0:T(8,128)(2,1)}), bf16[1536,1536]{1,0:T(8,128)(2,1)}) %all-gather.26.cloned.1.call-update) | async-done | bytes 4718608 | tf_op jit(solution)/shard_map/all_gather | solution.py:57
  369.4 9.8 copy.175
  412.5 7.0 convert_reduce_fusion.3
  430.7 7.7 fusion.66
  438.4 19.2 %convert_reduce_fusion.4 = (f32[12,64]{1,0:T(8,128)S(1)}, bf16[12,64,512]{2,1,0:T(8,128)(2,1)}) fusion(bf16[512,12,64]{0,2,1:T(8,128)(2,1)} %bitcast.224, f32[12,512,512]{1,2,0:T(8,128)} %fusion.66, f32[12,512,512]{1,2,0:T(8,128)} %get-tuple-element.39, f32[12,512]{1,0:T(8,128)S(1)} %get-tuple-element.38), kind=kOutput, calls=%fused_computation.38 | convolution fusion | flops 425858816 | bytes 26766336 | tf_op jit(solution)/shard_map/hqk,khd->qhd/dot_general | solution.py:184
  469.3 18.7 %fusion.38 = bf16[12,64,512]{2,1,0:T(8,128)(2,1)} fusion(bf16[512,12,64]{0,2,1:T(8,128)(2,1)} %bitcast.221, f32[12,512,512]{1,2,0:T(8,128)} %fusion.66, f32[12,512,512]{1,2,0:T(8,128)} %get-tuple-element.39, f32[12,512]{1,0:T(8,128)S(1)} %get-tuple-element.38), kind=kOutput, calls=%fused_computation.70 | convolution fusion | flops 425073152 | bytes 26763264 | tf_op jit(solution)/shard_map/hqk,qhd->khd/dot_general | solution.py:185
  506.1 11.7 %convert_element_type.259 = bf16[16,48,2,1536]{3,2,1,0:T(2,128)(2,1)} reshape(bf16[768,3072]{1,0:T(8,128)(2,1)} %convolution_convert_fusion.1) | data formatting | bytes 9437184 | tf_op jit(solution)/shard_map/convert_element_type | solution.py:65
  531.1 11.7 %convert_element_type.264 = bf16[16,48,2,1536]{3,2,1,0:T(2,128)(2,1)} reshape(bf16[768,3072]{1,0:T(8,128)(2,1)} %convolution_convert_fusion) | data formatting | bytes 9437184 | tf_op jit(solution)/shard_map/convert_element_type | solution.py:65
  566.8 10.9 %all-to-all-done.1.src = bf16[32,16,768]{2,1,0:T(8,128)(2,1)S(1)} async-done(((bf16[32,16,768]{2,1,0:T(8,128)(2,1)}), bf16[32,16,768]{2,1,0:T(8,128)(2,1)S(1)}, u32[]{:S(2)}, u32[]{:S(2)}) %all-to-all-start.1) | async-done | bytes 786464 | tf_op jit(solution)/shard_map/all_to_all | solution.py:108
  581.3 25.9 %pick.2 = bf16[32,16,768]{2,1,0:T(8,128)(2,1)} custom-call(s32[32]{0:T(128)} %order.1, bf16[32,16,768]{2,1,0:T(8,128)(2,1)} %copy-done.4), custom_call_target="tpu_custom_call" | custom-call | tf_op jit(solution)/shard_map/pick/pallas_call | solution.py:81
  611.3 42.3 %psum.7 = f32[9216]{0:T(1024)S(1)} all-reduce(f32[9216]{0:T(1024)S(1)} %constant_dynamic-update-slice_fusion), channel_id=1, replica_groups=mesh['dp'=16,'tensor'=2] {'dp','tensor'}, use_global_device_ids=true, to_apply=%region_27.28 | all-reduce | flops 9216 | bytes 73728 | tf_op jit(solution)/shard_map/psum | solution.py:206
  661.7 48.6 %reduce-scatter.7.cloned.1.call-done = bf16[48,384]{1,0:T(8,128)(2,1)} async-done(((bf16[1536,384]{1,0:T(8,128)(2,1)}), bf16[48,384]{1,0:T(8,128)(2,1)}) %reduce-scatter.7.cloned.1.call-update) | async-done | bytes 36880 | tf_op jit(solution)/shard_map/reduce_scatter | solution.py:66
  711.7 98.8 %reduce-scatter.9.cloned.1.call-done = bf16[48,384]{1,0:T(8,128)(2,1)} async-done(((bf16[1536,384]{1,0:T(8,128)(2,1)}), bf16[48,384]{1,0:T(8,128)(2,1)}) %reduce-scatter.9.cloned.1.call-update) | async-done | bytes 36880 | tf_op jit(solution)/shard_map/reduce_scatter | solution.py:66
  812.9 109.2 %reduce-scatter.15.cloned.1.call-done = bf16[48,1536]{1,0:T(8,128)(2,1)} async-done(((bf16[1536,1536]{1,0:T(8,128)(2,1)}), bf16[48,1536]{1,0:T(8,128)(2,1)}) %reduce-scatter.15.cloned.1.call-update) | async-done | bytes 147472 | tf_op jit(solution)/shard_map/reduce_scatter | solution.py:66
  923.7 110.7 %reduce-scatter.17.cloned.1.call-done = bf16[48,1536]{1,0:T(8,128)(2,1)} async-done(((bf16[1536,1536]{1,0:T(8,128)(2,1)}), bf16[48,1536]{1,0:T(8,128)(2,1)}) %reduce-scatter.17.cloned.1.call-update) | async-done | bytes 147472 | tf_op jit(solution)/shard_map/reduce_scatter | solution.py:66
  (230 shorter events, 200.2 us)
Async XLA Ops:
  7.2 89.5 %all-gather.18.cloned.1.call-start = ((), (), s32[]{:S(2)}) async-start(), calls=%async_computation.19 | async-start | bytes 1216512 | tf_op jit(solution)/shard_map/all_gather | solution.py:57
  7.9 117.3 %all-gather.20.cloned.1.call-start = ((), (), s32[]{:S(2)}) async-start(), calls=%async_computation.20 | async-start | bytes 1216512 | tf_op jit(solution)/shard_map/all_gather | solution.py:57
  8.7 172.6 %all-gather.16.cloned.1.call-start = ((), (), s32[]{:S(2)}) async-start(), calls=%async_computation.18 | async-start | bytes 1216512 | tf_op jit(solution)/shard_map/all_gather | solution.py:57
  9.4 229.4 %all-gather.22.cloned.1.call-start = ((), (), s32[]{:S(2)}) async-start(), calls=%async_computation.21 | async-start | bytes 1216512 | tf_op jit(solution)/shard_map/all_gather | solution.py:57
  10.0 294.2 %all-gather.24.cloned.1.call-start = ((), (), s32[]{:S(2)}) async-start(), calls=%async_computation.22 | async-start | bytes 4866048 | tf_op jit(solution)/shard_map/all_gather | solution.py:57
  10.6 358.9 %all-gather.26.cloned.1.call-start = ((), (), s32[]{:S(2)}) async-start(), calls=%async_computation.23 | async-start | bytes 4866048 | tf_op jit(solution)/shard_map/all_gather | solution.py:57
  12.4 32.1 %copy-start.31 = (s32[32]{0:T(128)S(1)}, s32[32]{0:T(128)}, u32[]{:S(2)}) copy-start(s32[32]{0:T(128)} %order.1) | copy-start | bytes 388
  12.4 32.1 %copy-start.29 = (f32[384]{0:T(512)S(1)}, f32[384]{0:T(512)}, u32[]{:S(2)}) copy-start(f32[384]{0:T(512)} %param.29) | copy-start | bytes 4612
  12.4 44.2 %copy-start.30 = (f32[384]{0:T(512)S(1)}, f32[384]{0:T(512)}, u32[]{:S(2)}) copy-start(f32[384]{0:T(512)} %param.30) | copy-start | bytes 4612
  12.4 49.1 %copy-start.25 = (f32[1536]{0:T(1024)S(1)}, f32[1536]{0:T(1024)}, u32[]{:S(2)}) copy-start(f32[1536]{0:T(1024)} %param.32) | copy-start | bytes 18436
  12.4 49.1 %copy-start.35 = (s32[32]{0:T(128)S(1)}, s32[32]{0:T(128)}, u32[]{:S(2)}) copy-start(s32[32]{0:T(128)} %param.21) | copy-start | bytes 388
  40.9 142.8 %all-to-all-start = ((bf16[2,256,768]{2,1,0:T(8,128)(2,1)}), bf16[2,256,768]{2,1,0:T(8,128)(2,1)S(1)}, u32[]{:S(2)}, u32[]{:S(2)}) async-start(bf16[2,256,768]{2,1,0:T(8,128)(2,1)} %param.19), calls=%async_computation | async-start | bytes 1572864 | tf_op jit(solution)/shard_map/all_to_all | solution.py:135
  99.1 89.1 %copy-start.9 = (bf16[96,8,2,384]{3,1,2,0:T(8,128)(2,1)}, bf16[96,8,2,384]{3,1,2,0:T(8,128)(2,1)S(1)}, u32[]{:S(2)}) copy-start(bf16[96,8,2,384]{3,1,2,0:T(8,128)(2,1)S(1)} %copy.202) | copy-start | bytes 3538948
  184.6 59.4 %all-to-all-start.4 = ((bf16[32,16,768]{2,1,0:T(8,128)(2,1)}), bf16[32,16,768]{2,1,0:T(8,128)(2,1)S(1)}, u32[]{:S(2)}, u32[]{:S(2)}) async-start(bf16[32,16,768]{2,1,0:T(8,128)(2,1)} %pick.3), calls=%async_computation.4 | async-start | bytes 1572864 | tf_op jit(solution)/shard_map/all_to_all | solution.py:99
  188.2 470.8 %reduce-scatter.13.cloned.1.call-start = ((), (), s32[]{:S(2)}) async-start(), calls=%async_computation.15 | async-start | bytes 1216512 | tf_op jit(solution)/shard_map/reduce_scatter | solution.py:66
  412.4 247.9 %reduce-scatter.11.cloned.1.call-start = ((), (), s32[]{:S(2)}) async-start(), calls=%async_computation.14 | async-start | bytes 1216512 | tf_op jit(solution)/shard_map/reduce_scatter | solution.py:66
  430.7 279.6 %reduce-scatter.7.cloned.1.call-start = ((), (), s32[]{:S(2)}) async-start(), calls=%async_computation.12 | async-start | bytes 1216512 | tf_op jit(solution)/shard_map/reduce_scatter | solution.py:66
  469.2 341.3 %reduce-scatter.9.cloned.1.call-start = ((), (), s32[]{:S(2)}) async-start(), calls=%async_computation.13 | async-start | bytes 1216512 | tf_op jit(solution)/shard_map/reduce_scatter | solution.py:66
  499.6 422.5 %reduce-scatter.15.cloned.1.call-start = ((), (), s32[]{:S(2)}) async-start(), calls=%async_computation.16 | async-start | bytes 4866048 | tf_op jit(solution)/shard_map/reduce_scatter | solution.py:66
  523.3 511.1 %reduce-scatter.17.cloned.1.call-start = ((), (), s32[]{:S(2)}) async-start(), calls=%async_computation.17 | async-start | bytes 4866048 | tf_op jit(solution)/shard_map/reduce_scatter | solution.py:66
  550.5 27.3 %all-to-all-start.1 = ((bf16[32,16,768]{2,1,0:T(8,128)(2,1)}), bf16[32,16,768]{2,1,0:T(8,128)(2,1)S(1)}, u32[]{:S(2)}, u32[]{:S(2)}) async-start(bf16[32,16,768]{2,1,0:T(8,128)(2,1)} %bitcast.22), calls=%async_computation.1 | async-start | bytes 1572864 | tf_op jit(solution)/shard_map/all_to_all | solution.py:108
  577.8 29.5 %all-to-all-start.5 = ((bf16[2,2,98304]{2,1,0:T(2,128)(2,1)}), bf16[2,2,98304]{2,1,0:T(2,128)(2,1)S(1)}, u32[]{:S(2)}, u32[]{:S(2)}) async-start(bf16[2,2,98304]{2,1,0:T(2,128)(2,1)} %reshape.303), calls=%async_computation.5 | async-start | bytes 1572864 | tf_op jit(solution)/shard_map/all_to_all | solution.py:189
  607.2 48.3 %copy-start.5 = (bf16[2,2,98304]{2,1,0:T(2,128)(2,1)}, bf16[2,2,98304]{2,1,0:T(2,128)(2,1)S(1)}, u32[]{:S(2)}) copy-start(bf16[2,2,98304]{2,1,0:T(2,128)(2,1)S(1)} %all-to-all-done.5) | copy-start | bytes 2359300
  607.2 204.7 %all-to-all-start.2 = ((bf16[32,16,768]{2,1,0:T(8,128)(2,1)}), bf16[32,16,768]{2,1,0:T(8,128)(2,1)S(1)}, u32[]{:S(2)}, u32[]{:S(2)}) async-start(bf16[32,16,768]{2,1,0:T(8,128)(2,1)} %pick.2), calls=%async_computation.2 | async-start | bytes 1572864 | tf_op jit(solution)/shard_map/all_to_all | solution.py:112
  (35 other events, 103.9 us)
Sparse Core Ops, SparseCore 0:
  10.9 58.1 all-gather.17
  72.0 53.1 all-gather.19
  128.1 53.0 all-gather.15
  184.0 54.7 all-gather.21
  241.6 62.5 all-gather.23
  306.9 62.4 all-gather.25
  412.5 94.9 reduce-scatter.12
  512.6 97.1 reduce-scatter.10
  615.0 95.2 reduce-scatter.6
  715.2 95.2 reduce-scatter.8
  816.0 106.0 reduce-scatter.14
  928.3 106.0 reduce-scatter.16

commit v2 on v1

v2 whole, which is shorter than its diff:
```python
import functools

import jax
import jax.numpy as jnp
from jax import lax
from jax.experimental import pallas as pl
from jax.experimental.pallas import tpu as pltpu
from jax.sharding import PartitionSpec as P

HEAD = 64
PAIR = 2 * HEAD
EPSILON = 1e-05
SQRT_HALF = 0.7071067811865476
INV_ROOT_TWO_PI = 0.3989422804014327
BOTH = ("dp", "tensor")
F32 = jnp.float32
BF16 = jnp.bfloat16
TILE = 256
ROWS = 128
HBM = pl.BlockSpec(memory_space=pl.ANY)
VMEM = pl.BlockSpec(memory_space=pltpu.VMEM)
SMEM = pl.BlockSpec(memory_space=pltpu.SMEM)
LEN, AT_Z, AT_X, AT_C, AT_Y = range(5)


def dot_nn(a, b):
    return lax.dot_general(a, b, (((1,), (0,)), ((), ())), preferred_element_type=F32)


def dot_nt(a, b):
    return lax.dot_general(a, b, (((1,), (1,)), ((), ())), preferred_element_type=F32)


def params(mib):
    return pltpu.CompilerParams(vmem_limit_bytes=mib << 20)


def exchange(value, bit):
    count = lax.axis_size("dp") * lax.axis_size("tensor")
    return lax.ppermute(value, BOTH, [(i, i ^ (1 << bit)) for i in range(count)])


def in_order(bit_at, mine, other, axis):
    low = jnp.where(bit_at == 0, mine, other)
    high = jnp.where(bit_at == 0, other, mine)
    return jnp.stack([low, high], axis=axis)


def gather_pieces(first, second, at):
    _, at_x, _, at_y, at_z0, at_z1 = at
    both = jnp.stack([first, second])
    both = in_order(at_z1, both, exchange(both, 4), 1)
    both = in_order(at_z0, both, exchange(both, 3), 2)
    both = both.reshape(2, 4, *first.shape)
    a, b = both[0], both[1]
    a = in_order(at_x, a, exchange(a, 2), 0)
    b = in_order(at_y, b, exchange(b, 0), 0)
    a_far, b_far = exchange(a, 0), exchange(b, 2)
    return [p for near in (a, a_far, b, b_far) for p in (near, exchange(near, 1))]


def load_pieces(scalars, pieces, weight, sems, spans):
    copies = []

    def add(src, dst):
        copies.append(pltpu.make_async_copy(src, dst, sems.at[len(copies)]))

    for number, piece in enumerate(pieces):
        half, far, other = number // 4, (number // 2) % 2, number % 2
        at_c = scalars[AT_C] ^ other
        for inner in range(2):
            if half == 0:
                at_x, at_y = inner, scalars[AT_Y] ^ far
            else:
                at_x, at_y = scalars[AT_X] ^ far, inner
            for start, width, to in spans[half]:
                column = pl.multiple_of(to(at_y), 128)
                add(
                    piece.at[inner, :, :, pl.ds(start, width)],
                    weight.at[:, at_x, at_c, :, pl.ds(column, width)],
                )
    return copies


def load_whole(scalars, pieces, weight, sems, spans):
    return [pltpu.make_async_copy(pieces[0], weight, sems.at[0])]


def normalize(z):
    mean = jnp.mean(z, axis=-1, keepdims=True)
    center = z - mean
    rscale = lax.rsqrt(jnp.mean(center * center, axis=-1, keepdims=True) + EPSILON)
    return center * rscale, rscale


def norm_backward(e, normal, rscale, gain):
    scaled = e * gain
    mean = jnp.mean(scaled, axis=-1, keepdims=True)
    tilt = jnp.mean(scaled * normal, axis=-1, keepdims=True)
    return rscale * (scaled - mean - normal * tilt)


def lane_mask(shape, odd):
    lane = lax.broadcasted_iota(jnp.int32, shape, len(shape) - 1)
    return (lane >= HEAD) if odd else (lane < HEAD)


def flat(weight):
    return weight.reshape(-1, weight.shape[-1])


def run_copies(copies):
    for c in copies:
        c.start()
    for c in copies:
        c.wait()


def attend_kernel(load, scalars, x_ref, vec_ref, *refs):
    pieces, refs = refs[:-11], refs[-11:]
    q_ref, k_ref, v_ref, att_ref, lse_ref, n_ref, r_ref, low_ref, w5, acc, sems = refs
    run_copies(load(scalars, pieces, w5, sems))
    w = flat(w5)
    seq, features = x_ref.shape
    live = lax.broadcasted_iota(jnp.int32, (1, seq), 1) < scalars[LEN]
    scale = HEAD**-0.5

    @pl.loop(0, features // TILE)
    def _(t):
        col = pl.multiple_of(t * TILE, TILE)
        here = pl.ds(col, TILE)
        x = x_ref[...]
        q = dot_nn(x, w[:, here]) + vec_ref[0:1, here]
        q_ref[:, here] = (q.astype(BF16).astype(F32) * scale).astype(BF16)
        k = dot_nn(x, w[:, pl.ds(pl.multiple_of(features + col, TILE), TILE)])
        k_ref[:, here] = k.astype(BF16)
        v = dot_nn(x, w[:, pl.ds(pl.multiple_of(2 * features + col, TILE), TILE)])
        v_ref[:, here] = (v + vec_ref[1:2, here]).astype(BF16)

    lse_ref[...] = jnp.zeros_like(lse_ref)

    @pl.loop(0, features // PAIR)
    def _(pair):
        here = pl.ds(pl.multiple_of(pair * PAIR, PAIR), PAIR)
        k2, v2 = k_ref[:, here], v_ref[:, here]
        keys = [jnp.where(lane_mask(k2.shape, odd), k2, jnp.zeros_like(k2)) for odd in range(2)]
        column = lax.broadcasted_iota(jnp.int32, (ROWS, 128), 1)
        for row in range(0, seq, ROWS):
            rows = pl.ds(row, ROWS)
            q2 = q_ref[rows, here]
            outs = []
            sums = lse_ref[rows, :]
            for odd in range(2):
                s = jnp.where(live, dot_nt(q2, keys[odd]), -1e9)
                top = jnp.max(s, axis=-1, keepdims=True)
                e = jnp.exp(s - top)
                total = jnp.sum(e, axis=-1, keepdims=True)
                outs.append(dot_nn((e * (1.0 / total)).astype(BF16), v2))
                sums = jnp.where(column == 2 * pair + odd, top + jnp.log(total), sums)
            lse_ref[rows, :] = sums
            att_ref[rows, here] = jnp.where(lane_mask(outs[0].shape, 1), outs[1], outs[0]).astype(BF16)

    @pl.loop(0, features // TILE)
    def _(t):
        col = pl.multiple_of(t * TILE, TILE)
        acc[:, pl.ds(col, TILE)] = dot_nt(att_ref[...], w[pl.ds(col, TILE), 3 * features :])

    @pl.loop(0, seq // ROWS)
    def _(t):
        rows = pl.ds(pl.multiple_of(t * ROWS, ROWS), ROWS)
        normal, rscale = normalize(x_ref[rows, :].astype(F32) + acc[rows, :] + vec_ref[2:3, :])
        n_ref[rows, :] = normal
        r_ref[rows, :] = rscale
        low_ref[rows, :] = (normal * vec_ref[3:4, :] + vec_ref[4:5, :]).astype(BF16)


def forward_kernel(load, scalars, low_ref, n_ref, vec_ref, up_bias_ref, *refs):
    pieces, refs = refs[:-10], refs[-10:]
    act_ref, slope_ref, n2_ref, r2_ref, out_ref, w5_up, w5_down, acc, sems, sems_down = refs
    half = len(pieces) // 2
    copies = load(scalars, pieces[:half], w5_up, sems)
    later = load(scalars, pieces[half:], w5_down, sems_down)
    for c in copies + later:
        c.start()
    for c in copies:
        c.wait()
    up, down = flat(w5_up), flat(w5_down)
    seq, features = low_ref.shape
    units = up.shape[1]

    @pl.loop(0, units // TILE)
    def _(t):
        here = pl.ds(pl.multiple_of(t * TILE, TILE), TILE)
        h = dot_nn(low_ref[...], up[:, here]) + up_bias_ref[0:1, here]
        phi = 0.5 + 0.5 * lax.erf(h * SQRT_HALF)
        act_ref[:, here] = (h * phi).astype(BF16)
        slope_ref[:, here] = (phi + h * jnp.exp(-0.5 * h * h) * INV_ROOT_TWO_PI).astype(slope_ref.dtype)

    for c in later:
        c.wait()

    @pl.loop(0, features // TILE)
    def _(t):
        col = pl.multiple_of(t * TILE, TILE)
        acc[:, pl.ds(col, TILE)] = dot_nt(act_ref[...], down[pl.ds(col, TILE), :])

    groups, parts, piece, _ = out_ref.shape
    block = seq // parts

    for part in range(parts):
        rows = pl.ds(part * block, block)
        normed = n_ref[rows, :] * vec_ref[0:1, :] + vec_ref[1:2, :]
        normal, rscale = normalize(normed + acc[rows, :] + vec_ref[2:3, :])
        n2_ref[rows, :] = normal
        r2_ref[rows, :] = rscale
        at = part * block + lax.broadcasted_iota(jnp.int32, (block, 1), 0)
        final = (normal * vec_ref[3:4, :] + vec_ref[4:5, :]) * (at < scalars[LEN]).astype(F32)
        out_ref[:, part] = final.astype(BF16).reshape(groups, piece, features)


def column_sum(value):
    return jnp.sum(value, axis=0, keepdims=True)


def down_kernel(store, scalars, cot_ref, n2_ref, r2_ref, act_ref, vec_ref, *refs):
    outs, (second_ref, low_ref, sums_ref, turned) = refs[:-4], refs[-4:]
    groups, parts, piece, features = cot_ref.shape
    block = groups * piece
    sums = [jnp.zeros((1, features), F32)] * 3
    for part in range(parts):
        rows = pl.ds(part * block, block)
        at = part * block + lax.broadcasted_iota(jnp.int32, (block, 1), 0)
        grad_out = cot_ref[:, part].reshape(block, features).astype(F32)
        grad_out = grad_out * (at < scalars[LEN]).astype(F32)
        normal = n2_ref[rows, :]
        second = norm_backward(grad_out, normal, r2_ref[rows, :], vec_ref[0:1, :])
        low = second.astype(BF16)
        second_ref[rows, :] = second
        low_ref[rows, :] = low
        turned[:, rows] = low.T
        more = [column_sum(low.astype(F32)), column_sum(grad_out * normal), column_sum(grad_out)]
        sums = [a + b for a, b in zip(sums, more)]
    sums_ref[...] = jnp.concatenate(sums, axis=0)
    units = act_ref.shape[1]

    @pl.loop(0, units // TILE)
    def _(t):
        here = pl.ds(pl.multiple_of(t * TILE, TILE), TILE)
        store(scalars, outs, t, dot_nn(turned[...], act_ref[:, here]).astype(BF16))


def up_kernel(load, store, kept, scalars, gffn_ref, second_ref, slope_ref, low_ref, n_ref, r_ref, vec_ref, *refs):
    pieces, refs = refs[:-kept], refs[-kept:]
    first_ref, gattn_ref, sums_ref, unit_sums_ref, *outs = refs[:-7]
    w5_up, w5_down, ghid, turned, acc, sems, sems_down = refs[-7:]
    half = len(pieces) // 2
    copies = load(scalars, pieces[half:], w5_down, sems_down)
    later = load(scalars, pieces[:half], w5_up, sems)
    for c in copies + later:
        c.start()
    up, down = flat(w5_up), flat(w5_down)
    seq, features = low_ref.shape
    units = slope_ref.shape[1]
    turned[...] = low_ref[...].T
    for c in copies:
        c.wait()

    @pl.loop(0, units // TILE)
    def _(t):
        here = pl.ds(pl.multiple_of(t * TILE, TILE), TILE)
        grad_act = dot_nn(gffn_ref[...], down[:, here])
        low = (grad_act * slope_ref[:, here].astype(F32)).astype(BF16)
        ghid[:, here] = low
        unit_sums_ref[0:1, here] = column_sum(low.astype(F32))
        store(scalars, outs, t, dot_nn(turned[...], low).astype(BF16))

    for c in later:
        c.wait()

    @pl.loop(0, features // TILE)
    def _(t):
        col = pl.multiple_of(t * TILE, TILE)
        acc[:, pl.ds(col, TILE)] = dot_nt(ghid[...], up[pl.ds(col, TILE), :])

    sums_ref[...] = jnp.zeros_like(sums_ref)

    @pl.loop(0, seq // ROWS)
    def _(t):
        rows = pl.ds(pl.multiple_of(t * ROWS, ROWS), ROWS)
        normal = n_ref[rows, :]
        e = acc[rows, :] + second_ref[rows, :]
        first = norm_backward(e, normal, r_ref[rows, :], vec_ref[0:1, :])
        low = first.astype(BF16)
        first_ref[rows, :] = first
        gattn_ref[rows, :] = low
        more = [column_sum(low.astype(F32)), column_sum(e * normal), column_sum(e)]
        sums_ref[...] += jnp.concatenate(more, axis=0)


def attend_back_kernel(load, store, kept, scalars, gattn_ref, first_ref, x_ref, q_ref, k_ref, v_ref, att_ref, lse_ref, *refs):
    pieces, refs = refs[:-kept], refs[-kept:]
    grad_ref, sums_ref, *outs = refs[:-11]
    w5, gatt, gq, gk, gv, turned, turned_q, turned_do, gkt, gvt, sems = refs[-11:]
    copies = load(scalars, pieces, w5, sems)
    for c in copies:
        c.start()
    w = flat(w5)
    seq, features = x_ref.shape
    scale = HEAD**-0.5
    live = lax.broadcasted_iota(jnp.int32, (1, seq), 1) < scalars[LEN]
    turned[...] = gattn_ref[...].T
    for c in copies:
        c.wait()

    @pl.loop(0, features // TILE)
    def _(t):
        col = pl.multiple_of(t * TILE, TILE)
        gatt[:, pl.ds(col, TILE)] = dot_nn(
            gattn_ref[...], w[:, pl.ds(pl.multiple_of(3 * features + col, TILE), TILE)]
        ).astype(BF16)

    store(scalars, outs, 3, dot_nn(turned[...], att_ref[...]).astype(BF16))
    turned[...] = x_ref[...].T

    @pl.loop(0, features // PAIR)
    def _(pair):
        here = pl.ds(pl.multiple_of(pair * PAIR, PAIR), PAIR)
        k2, v2 = k_ref[:, here], v_ref[:, here]
        keys = [jnp.where(lane_mask(k2.shape, odd), k2, jnp.zeros_like(k2)) for odd in range(2)]
        values = [jnp.where(lane_mask(v2.shape, odd), v2, jnp.zeros_like(v2)) for odd in range(2)]
        turned_q[...] = q_ref[:, here].T
        turned_do[...] = gatt[:, here].T
        column = lax.broadcasted_iota(jnp.int32, (ROWS, 128), 1)
        for row in range(0, seq, ROWS):
            rows = pl.ds(row, ROWS)
            q2, do2 = q_ref[rows, here], gatt[rows, here]
            both = do2.astype(F32) * att_ref[rows, here].astype(F32)
            sums = lse_ref[rows, :]
            outs_q = []
            for odd in range(2):
                head = pl.ds(odd * HEAD, HEAD)
                lse = jnp.sum(jnp.where(column == 2 * pair + odd, sums, 0.0), axis=-1, keepdims=True)
                inner = jnp.sum(jnp.where(lane_mask(both.shape, odd), both, 0.0), axis=-1, keepdims=True)
                s = jnp.where(live, dot_nt(q2, keys[odd]), -1e9)
                p = jnp.exp(s - lse)
                gs = (p * (dot_nt(do2, values[odd]) - inner)).astype(BF16)
                outs_q.append(dot_nn(gs, k2))
                gkt_part = dot_nn(turned_q[head, rows], gs)
                gvt_part = dot_nn(turned_do[head, rows], p.astype(BF16))
                if row == 0:
                    gkt[head, :] = gkt_part
                    gvt[head, :] = gvt_part
                else:
                    gkt[head, :] += gkt_part
                    gvt[head, :] += gvt_part
            gq[rows, here] = (
                jnp.where(lane_mask(outs_q[0].shape, 1), outs_q[1], outs_q[0]) * scale
            ).astype(BF16)
        gk[:, here] = gkt[...].astype(BF16).T
        gv[:, here] = gvt[...].astype(BF16).T

    store(scalars, outs, 0, dot_nn(turned[...], gq[...]).astype(BF16))
    store(scalars, outs, 1, dot_nn(turned[...], gk[...]).astype(BF16))
    store(scalars, outs, 2, dot_nn(turned[...], gv[...]).astype(BF16))
    sums_ref[...] = jnp.concatenate(
        [column_sum(gq[...].astype(F32)), column_sum(gv[...].astype(F32))], axis=0
    )
    parts, block, _ = grad_ref.shape

    @pl.loop(0, features // TILE)
    def _(t):
        col = pl.multiple_of(t * TILE, TILE)
        here = pl.ds(col, TILE)
        total = (
            first_ref[:, here]
            + dot_nt(gq[...], w[here, 0:features])
            + dot_nt(gk[...], w[here, features : 2 * features])
            + dot_nt(gv[...], w[here, 2 * features : 3 * features])
        ).astype(BF16)
        for part in range(parts):
            grad_ref[part, :, here] = total[part * block : (part + 1) * block]


def each_block(scalars, outs, write):
    keep, send = outs
    for mine in range(2):

        @pl.when(scalars[AT_C] == mine)
        def _():
            for at_z in range(4):
                for at_x in range(2):
                    write(at_z, at_x, mine, keep)
                    write(at_z, at_x, 1 - mine, send)


def store_units(scalars, outs, t, value):
    rows, width = outs[0].shape[-2:]
    tiles = width // TILE
    half, col = (t // tiles) % 2, pl.multiple_of((t % tiles) * TILE, TILE)
    far_y = (t // (2 * tiles)) ^ scalars[AT_Y]

    def write(at_z, at_x, at_c, out):
        far_z, far_x = at_z ^ scalars[AT_Z], at_x ^ scalars[AT_X]
        one = jnp.where(half == 0, far_x, far_y)
        two = jnp.where(half == 0, far_y, far_x)
        start = ((at_z * 2 + at_x) * 2 + at_c) * rows
        out[half, one, two, far_z, :, pl.ds(col, TILE)] = value[start : start + rows]

    each_block(scalars, outs, write)


def store_heads(scalars, outs, number, value):
    rows, width = outs[0].shape[-2:]
    cols = width // 2
    half, col = number // 2, (number % 2) * cols

    def write(at_z, at_x, at_c, out):
        far_z, far_x = at_z ^ scalars[AT_Z], at_x ^ scalars[AT_X]
        start = ((at_z * 2 + at_x) * 2 + at_c) * rows
        for at_y in range(2):
            far_y = at_y ^ scalars[AT_Y]
            one, two = (far_x, far_y) if half == 0 else (far_y, far_x)
            piece = value[start : start + rows, at_y * cols : (at_y + 1) * cols]
            out[half, one, two, far_z, :, col : col + cols] = piece

    each_block(scalars, outs, write)


def store_units_whole(scalars, outs, t, value):
    outs[0][:, pl.ds(pl.multiple_of(t * TILE, TILE), TILE)] = value


def store_heads_whole(scalars, outs, number, value):
    cols = value.shape[1]
    outs[0][:, number * cols : (number + 1) * cols] = value


def pick_kernel(order, src, dst):
    @pl.loop(0, dst.shape[0])
    def _(t):
        dst[t] = src[order[t]]


def pick(pieces, order):
    return pl.pallas_call(
        pick_kernel,
        out_shape=jax.ShapeDtypeStruct(pieces.shape, pieces.dtype),
        in_specs=[SMEM, VMEM],
        out_specs=VMEM,
        compiler_params=params(8),
        name="pick",
    )(order, pieces)


def add_low(a, b):
    return (a.astype(F32) + b.astype(F32)).astype(BF16)


def scatter_pieces(keep, send):
    near = exchange(send, 1)
    a_send = add_low(keep[0, 1], near[0, 1])
    b_send = add_low(keep[1, 1], near[1, 1])
    a_far, b_far = exchange(a_send, 2), exchange(b_send, 0)
    a_keep = add_low(keep[0, 0], near[0, 0])
    b_keep = add_low(keep[1, 0], near[1, 0])
    a_next = exchange(add_low(a_keep[1], a_far[1]), 0)
    b_next = exchange(add_low(b_keep[1], b_far[1]), 2)
    a_keep, b_keep = add_low(a_keep[0], a_far[0]), add_low(b_keep[0], b_far[0])
    rows, width = keep.shape[-2:]
    both = jnp.stack([add_low(a_keep, a_next), add_low(b_keep, b_next)]).reshape(2, 2, 2, rows, width)
    far = exchange(both[:, :, 1], 3)
    both = add_low(both[:, :, 0], far)
    far = exchange(both[:, 1], 4)
    total = both[:, 0].astype(F32) + far.astype(F32)
    return total[0], total[1]


def scatter_whole(grad, rows, cols):
    size = lax.axis_size("tensor")
    parts = grad.reshape(-1, rows, size, cols).transpose(0, 2, 1, 3).reshape(-1, cols)
    return lax.psum_scatter(parts, BOTH, scatter_dimension=0, tiled=True).astype(F32)


def gather_whole(shard):
    size = lax.axis_size("tensor")
    rows, cols = shard.shape
    got = lax.all_gather(shard, BOTH, axis=0, tiled=False).reshape(-1, size, rows, cols)
    return got.transpose(0, 2, 1, 3).reshape(1, 1, 1, -1, size * cols)


def deal(block, order):
    micro, half, features = block.shape
    dp, size = lax.axis_size("dp"), lax.axis_size("tensor")
    piece = half // dp
    pieces = block.reshape(micro, dp, piece, features).transpose(1, 0, 2, 3)
    spread = lax.all_to_all(pieces.reshape(dp, micro * piece, features), "dp", split_axis=0, concat_axis=0, tiled=True)
    chosen = pick(spread.reshape(dp * micro, piece, features), order)
    got = lax.all_to_all(chosen, BOTH, split_axis=0, concat_axis=0, tiled=True)
    return got.reshape(dp, size, piece, features)


def collect(pieces, order, micro):
    dp, size, piece, features = pieces.shape
    got = lax.all_to_all(pieces.reshape(dp * size, piece, features), BOTH, split_axis=0, concat_axis=0, tiled=True)
    chosen = pick(got, order).reshape(dp, micro * piece, features)
    back = lax.all_to_all(chosen, "dp", split_axis=0, concat_axis=0, tiled=True)
    return back.reshape(dp, micro, piece, features).transpose(1, 0, 2, 3).reshape(micro, dp * piece, features)


def on_device(
    tokens, cotangent, lengths, slot_order,
    query_weight, key_weight, value_weight, out_weight, up_weight, down_weight,
    query_bias, value_bias, out_bias, up_bias, down_bias,
    first_gain, first_offset, second_gain, second_offset,
):
    micro, half, features = tokens.shape
    dp, size = lax.axis_size("dp"), lax.axis_size("tensor")
    assert micro == size == 2
    dp_pos, at_y = lax.axis_index("dp"), lax.axis_index("tensor")
    rows, cols = query_weight.shape
    unit_cols = up_weight.shape[1]
    units = unit_cols * size
    seq = half * size
    slots = slot_order.shape[0]
    inverse = jnp.zeros_like(slot_order).at[slot_order].set(jnp.arange(slots, dtype=jnp.int32))
    at_c, at_x, at_z0, at_z1 = dp_pos & 1, (dp_pos >> 1) & 1, (dp_pos >> 2) & 1, dp_pos >> 3
    scalars = jnp.stack([lengths[dp_pos * size + at_y], dp_pos >> 2, at_x, at_c, at_y]).astype(jnp.int32)

    split = dp == 16 and rows % 16 == 0
    if split:
        dims = (4, 2, 2, rows)
        at = (at_c, at_x, None, at_y, at_z0, at_z1)
        heads_in = gather_pieces(
            jnp.concatenate([query_weight, key_weight], axis=1),
            jnp.concatenate([value_weight, out_weight], axis=1), at,
        )
        wide = unit_cols // 2
        up_in = gather_pieces(up_weight[:, :wide], up_weight[:, wide:], at)
        down_in = gather_pieces(down_weight[:, :wide], down_weight[:, wide:], at)
        unit_spans = [[(0, wide, lambda y, h=h: y * unit_cols + h * wide)] for h in range(2)]
        head_spans = [
            [(m * cols, cols, lambda y, n=2 * h + m: n * features + y * cols) for m in range(2)] for h in range(2)
        ]
        load_units = functools.partial(load_pieces, spans=unit_spans)
        load_heads = functools.partial(load_pieces, spans=head_spans)
        put_units, put_heads = store_units, store_heads
        grad_out = [jax.ShapeDtypeStruct((2, 2, 2, 4, rows, wide), BF16)] * 2
        count = 16
    else:
        dims = (1, 1, 1, features)
        heads_in = [jnp.concatenate(
            [gather_whole(w) for w in (query_weight, key_weight, value_weight, out_weight)], axis=-1
        )]
        up_in, down_in = [gather_whole(up_weight)], [gather_whole(down_weight)]
        load_units = load_heads = functools.partial(load_whole, spans=None)
        put_units, put_heads = store_units_whole, store_heads_whole
        grad_out = [jax.ShapeDtypeStruct((features, units), BF16)]
        count = 1

    own_half = lax.dynamic_index_in_dim(tokens, at_y, 0, keepdims=False)
    other_half = exchange(lax.dynamic_index_in_dim(tokens, 1 - at_y, 0, keepdims=False), 0)
    x = in_order(at_y, own_half, other_half, 0).reshape(seq, features)
    biases = jnp.concatenate([query_bias, value_bias, up_bias]).reshape(-1, cols)
    biases = in_order(at_y, biases, exchange(biases, 0), 1)
    biases = biases.reshape(-1, size, cols)
    full_query, full_value = biases[0].reshape(-1), biases[1].reshape(-1)
    full_up = biases[2:].transpose(1, 0, 2).reshape(1, units)

    cot = deal(cotangent, inverse)
    if not split:
        cot = cot.transpose(1, 0, 2, 3).reshape(1, size, half, features)

    def act(shape, dtype=BF16):
        return jax.ShapeDtypeStruct(shape, dtype)

    wide_rows, tall = act((seq, features)), act((seq, features), F32)
    column = act((seq, 1), F32)
    head_vec = jnp.stack([full_query, full_value, out_bias, first_gain, first_offset])
    sem = pltpu.SemaphoreType.DMA

    q, k, v, att, lse, n1, r1, low = pl.pallas_call(
        functools.partial(attend_kernel, load_heads),
        out_shape=(wide_rows, wide_rows, wide_rows, wide_rows, act((seq, 128), F32), tall, column, wide_rows),
        in_specs=[SMEM, VMEM, VMEM] + [HBM] * len(heads_in),
        out_specs=(VMEM,) * 8,
        scratch_shapes=[
            pltpu.VMEM((*dims, 4 * features), BF16), pltpu.VMEM((seq, features), F32), sem((2 * count,)),
        ],
        compiler_params=params(40),
        name="attend",
    )(scalars, x, head_vec, *heads_in)

    forward_vec = jnp.stack([first_gain, first_offset, down_bias, second_gain, second_offset])
    deal_dims = (dp, size, half // dp, features) if split else (1, size, half, features)
    wide_units = act((seq, units))
    active, slope, n2, r2, out = pl.pallas_call(
        functools.partial(forward_kernel, load_units),
        out_shape=(wide_units, wide_units, tall, column, act(deal_dims)),
        in_specs=[SMEM] + [VMEM] * 4 + [HBM] * (2 * len(up_in)),
        out_specs=(VMEM,) * 5,
        scratch_shapes=[
            pltpu.VMEM((*dims, units), BF16), pltpu.VMEM((*dims, units), BF16),
            pltpu.VMEM((seq, features), F32), sem((count,)), sem((count,)),
        ],
        compiler_params=params(40),
        name="forward",
    )(scalars, low, n1, forward_vec, full_up, *up_in, *down_in)
    if not split:
        out = out.reshape(size, dp, half // dp, features).transpose(1, 0, 2, 3)
    layer_out = collect(out, slot_order, micro)

    *down_grad, second, gffn, down_sums = pl.pallas_call(
        functools.partial(down_kernel, put_units),
        out_shape=(*grad_out, tall, wide_rows, act((3, features), F32)),
        in_specs=[SMEM] + [VMEM] * 5,
        out_specs=(VMEM,) * (len(grad_out) + 3),
        scratch_shapes=[pltpu.VMEM((features, seq), BF16)],
        compiler_params=params(40),
        name="down",
    )(scalars, cot, n2, r2, active, second_gain[None])

    first, gattn, up_sums, unit_sums, *up_grad = pl.pallas_call(
        functools.partial(up_kernel, load_units, put_units, 11 + len(grad_out)),
        out_shape=(tall, wide_rows, act((3, features), F32), act((1, units), F32), *grad_out),
        in_specs=[SMEM] + [VMEM] * 7 + [HBM] * (2 * len(up_in)),
        out_specs=(VMEM,) * (4 + len(grad_out)),
        scratch_shapes=[
            pltpu.VMEM((*dims, units), BF16), pltpu.VMEM((*dims, units), BF16),
            pltpu.VMEM((seq, units), BF16), pltpu.VMEM((features, seq), BF16),
            pltpu.VMEM((seq, features), F32), sem((count,)), sem((count,)),
        ],
        compiler_params=params(48),
        name="up",
    )(scalars, gffn, second, slope, low, n1, r1, first_gain[None], *up_in, *down_in)

    grad_rows, head_sums, *head_grad = pl.pallas_call(
        functools.partial(attend_back_kernel, load_heads, put_heads, 13 + len(grad_out)),
        out_shape=(act((size, half, features)), act((2, features), F32), *grad_out),
        in_specs=[SMEM] + [VMEM] * 8 + [HBM] * len(heads_in),
        out_specs=(VMEM,) * (2 + len(grad_out)),
        scratch_shapes=[
            pltpu.VMEM((*dims, 4 * features), BF16),
            *[pltpu.VMEM((seq, features), BF16)] * 4,
            pltpu.VMEM((features, seq), BF16),
            pltpu.VMEM((PAIR, seq), BF16), pltpu.VMEM((PAIR, seq), BF16),
            pltpu.VMEM((PAIR, seq), F32), pltpu.VMEM((PAIR, seq), F32), sem((2 * count,)),
        ],
        compiler_params=params(48),
        name="attend_back",
    )(scalars, gattn, first, x, q, k, v, att, lse, *heads_in)

    own_grad = lax.dynamic_index_in_dim(grad_rows, at_y, 0, keepdims=False)
    other_grad = exchange(lax.dynamic_index_in_dim(grad_rows, 1 - at_y, 0, keepdims=False), 0)
    input_grad = in_order(at_y, own_grad, other_grad, 0)

    if split:
        grads = []
        for pair in (head_grad,):
            a, b = scatter_pieces(*pair)
            grads += [a[:, :cols], a[:, cols:], b[:, :cols], b[:, cols:]]
        grads += [jnp.concatenate(scatter_pieces(*pair), axis=1) for pair in (up_grad, down_grad)]
    else:
        cut = [head_grad[0][:, n * features : (n + 1) * features] for n in range(4)]
        grads = [scatter_whole(g, rows, cols) for g in cut]
        grads += [scatter_whole(g[0], rows, unit_cols) for g in (up_grad, down_grad)]

    sums = jnp.concatenate([down_sums, up_sums, head_sums, unit_sums.reshape(-1, features)])
    if split:
        for bit in range(5):
            sums = sums + exchange(sums, bit)
    else:
        sums = lax.psum(sums, BOTH)

    def own(vec, width):
        return lax.dynamic_slice_in_dim(vec, at_y * width, width)

    return (
        layer_out, input_grad, *grads,
        own(sums[6], cols), own(sums[7], cols), sums[3], own(sums[8:].reshape(-1), unit_cols), sums[0],
        sums[4], sums[5], sums[1], sums[2],
    )


def solution(mesh):
    rows = P("dp", "tensor", None)
    weight = P("dp", "tensor")
    cut = P("tensor")
    whole = P()
    return jax.shard_map(
        on_device,
        mesh=mesh,
        in_specs=(rows, rows, whole, whole, *(weight,) * 6, cut, cut, whole, cut, *(whole,) * 5),
        out_specs=(rows, rows, *(weight,) * 6, cut, cut, whole, cut, *(whole,) * 5),
        check_vma=False,
    )
```

time: 1050 us -> 400 us (0.38)
  waiting for transfers between devices: 594 us -> 157 us
  matrix products: 119 us -> 0 us
  local copies, waits for them, and re-layouts: 131 us -> 31.8 us
  blocking collectives: 91.5 us -> 0 us
  starting transfers between devices: 18.4 us -> 80.2 us
  Pallas kernels: 51.8 us -> 106 us
  between operations: 15.2 us -> 2.02 us
    reduce_scatter x6 -> x0, waiting for transfers between devices: 367 us -> none  [scatter_grad(): lax.psum_scatter(parts, BOTH, scatter_dimension=0, tiled=True).astype(F32)]
    all_gather x6 -> x0, waiting for transfers between devices: 212 us -> none  [gather_weight(): got = lax.all_gather(shard, BOTH, axis=0, tiled=False)]
    ppermute x0 -> x59, waiting for transfers between devices: none -> 157 us  [exchange(): return lax.ppermute(value, BOTH, [(i, i ^ 1 << bit) for i in range(count)])]
    dot_general x23 -> x0, matrix products: 111 us -> none  [the longest x6 24.3 us: dot_tn(): lax.dot_general(a, b, (((0,), (0,)), ((), ())), preferred_element_type=F32)]
    pallas_call x0 -> x5, Pallas kernels: none -> 103 us  [the longest x1 29.4 us: on_device(): pl.pallas_call(functools.partial(attend_back_kernel, load_heads, put_head...]
    convert_element_type x18 -> x0, local copies, waits for them, and re-layouts: 67.5 us -> none  [the longest x13 59.6 us: scatter_grad(): parts = parts.reshape(-1, cols).astype(BF16)]
    ppermute x0 -> x59, starting transfers between devices: none -> 61.4 us  [exchange(): return lax.ppermute(value, BOTH, [(i, i ^ 1 << bit) for i in range(count)])]
    pallas_call x2, Pallas kernels: 51.8 us -> 3.31 us  [pick(): pl.pallas_call(pick_kernel, out_shape=jax.ShapeDtypeStruct(pieces.shape,...]
  transfers between devices with their start and end apart: 17 -> 63, of which waited for: 10 -> 33; matrix products, arithmetic and copies ran while one was open for 21% -> 7% of each run, Pallas kernels for 5% -> 27%
where the time goes in v2:
time: 400 us; the launch traced here: 399 us
  waiting for transfers between devices  157 us (39%)
  Pallas kernels  106 us (26%)
  starting transfers between devices  80.2 us (20%)
  local copies, waits for them, and re-layouts  31.8 us (8%)
  other arithmetic  22 us (6%)
    ppermute x59, waiting for transfers between devices, exchange(): return lax.ppermute(value, BOTH, [(i, i ^ 1 << bit) for i in range(count)])  157 us
    ppermute x59, starting transfers between devices, exchange(): return lax.ppermute(value, BOTH, [(i, i ^ 1 << bit) for i in range(count)])  61.4 us
    pallas_call x1, Pallas kernels, on_device(): pl.pallas_call(functools.partial(attend_back_kernel, load_heads, put_head...  29.4 us
    pallas_call x1, Pallas kernels, on_device(): pl.pallas_call(functools.partial(up_kernel, load_units, put_units, 11 + l...  25.6 us
    pallas_call x1, Pallas kernels, on_device(): pl.pallas_call(functools.partial(attend_kernel, load_heads), out_shape=(w...  25 us
    unnamed x133, local copies, waits for them, and re-layouts  22.2 us
    pallas_call x1, Pallas kernels, on_device(): pl.pallas_call(functools.partial(forward_kernel, load_units), out_shape=(...  14.1 us
    convert_element_type x18, other arithmetic, add_low(): return (a.astype(F32) + b.astype(F32)).astype(BF16)  11.6 us
  transfers between devices with their start and end apart: 63, of which 33 were waited for; matrix products, arithmetic and copies ran while one was open for 7% of the time, Pallas kernels for 27%

profile of v2, /device:TPU:0, one launch (start us, length us, event | category | flops | bytes accessed | tf_op | source)
XLA Modules:
  0.0 399.1 jit_solution(4583566378615770245)
XLA Ops:
  1.6 4.1 %collective-permute-start.2 = (bf16[2,48,768]{2,1,0:T(8,128)(2,1)S(1)}, bf16[2,48,768]{2,1,0:T(8,128)(2,1)S(1)}, u32[]{:S(2)}, u32[]{:S(2)}) collective-permute-start(bf16[2,48,768]{2,1,0:T(8,128)(2,1)S(1)} %pad_maximum_fusion.19), channel_id=1, source_target_pairs={{0,16},{1,17},{2,18},{3,19},{4,20},{5,21},{6,22},{7,23},{8,24},{9,... | collective-permute-start | bytes 442376 | tf_op jit(solution)/shard_map/ppermute | solution.py:40
  14.9 8.9 %collective-permute-done.2 = bf16[2,48,768]{2,1,0:T(8,128)(2,1)S(1)} collective-permute-done((bf16[2,48,768]{2,1,0:T(8,128)(2,1)S(1)}, bf16[2,48,768]{2,1,0:T(8,128)(2,1)S(1)}, u32[]{:S(2)}, u32[]{:S(2)}) %collective-permute-start.2) | collective-permute-done | bytes 147488 | tf_op jit(solution)/shard_map/ppermute | solution.py:40
  24.2 7.4 %collective-permute-done.22 = bf16[2,48,768]{2,1,0:T(8,128)(2,1)S(1)} collective-permute-done((bf16[2,48,768]{2,1,0:T(8,128)(2,1)S(1)}, bf16[2,48,768]{2,1,0:T(8,128)(2,1)S(1)}, u32[]{:S(2)}, u32[]{:S(2)}) %collective-permute-start.22) | collective-permute-done | bytes 147488 | tf_op jit(solution)/shard_map/ppermute | solution.py:40
  35.0 9.4 %collective-permute-done.3 = bf16[2,2,48,768]{3,2,0,1:T(8,128)(2,1)S(1)} collective-permute-done((bf16[2,2,48,768]{3,2,0,1:T(8,128)(2,1)S(1)}, bf16[2,2,48,768]{3,2,0,1:T(8,128)(2,1)S(1)}, u32[]{:S(2)}, u32[]{:S(2)}) %collective-permute-start.3) | collective-permute-done | bytes 294944 | tf_op jit(solution)/shard_map/ppermute | solution.py:40
  52.4 4.5 %collective-permute-done.13 = bf16[2,2,48,768]{3,2,0,1:T(8,128)(2,1)S(1)} collective-permute-done((bf16[2,2,48,768]{3,2,0,1:T(8,128)(2,1)S(1)}, bf16[2,2,48,768]{3,2,0,1:T(8,128)(2,1)S(1)}, u32[]{:S(2)}, u32[]{:S(2)}) %collective-permute-start.13) | collective-permute-done | bytes 294944 | tf_op jit(solution)/shard_map/ppermute | solution.py:40
  70.2 4.8 %collective-permute-done.18 = bf16[4,48,768]{2,1,0:T(8,128)(2,1)S(1)} collective-permute-done((bf16[4,48,768]{2,1,0:T(8,128)(2,1)S(1)}, bf16[4,48,768]{2,1,0:T(8,128)(2,1)S(1)}, u32[]{:S(2)}, u32[]{:S(2)}) %collective-permute-start.18) | collective-permute-done | bytes 294944 | tf_op jit(solution)/shard_map/ppermute | solution.py:40
  77.5 17.6 %collective-permute-done.1 = f32[6,384]{1,0:T(8,128)S(1)} collective-permute-done((f32[6,384]{1,0:T(8,128)S(1)}, f32[6,384]{1,0:T(8,128)S(1)}, u32[]{:S(2)}, u32[]{:S(2)}) %collective-permute-start.1) | collective-permute-done | bytes 9248 | tf_op jit(solution)/shard_map/ppermute | solution.py:40
  118.0 12.5 %collective-permute-done.20.refs_6_ = bf16[2,4,48,768]{3,2,1,0:T(8,128)(2,1)} collective-permute-done((bf16[2,4,48,768]{3,2,1,0:T(8,128)(2,1)S(1)}, bf16[2,4,48,768]{3,2,1,0:T(8,128)(2,1)}, u32[]{:S(2)}, u32[]{:S(2)}) %collective-permute-start.20) | collective-permute-done | bytes 589856 | tf_op jit(solution)/shard_map/ppermute | solution.py:40
  133.9 9.3 %collective-permute-done.30.refs_14_ = bf16[2,4,48,768]{3,2,1,0:T(8,128)(2,1)} collective-permute-done((bf16[2,4,48,768]{3,2,1,0:T(8,128)(2,1)}, bf16[2,4,48,768]{3,2,1,0:T(8,128)(2,1)}, u32[]{:S(2)}, u32[]{:S(2)}) %collective-permute-start.30) | collective-permute-done | bytes 589856 | tf_op jit(solution)/shard_map/ppermute | solution.py:40
  146.7 25.0 %attend.1 = (bf16[512,768]{1,0:T(8,128)(2,1)S(1)}, bf16[512,768]{1,0:T(8,128)(2,1)S(1)}, bf16[512,768]{1,0:T(8,128)(2,1)S(1)}, bf16[512,768]{1,0:T(8,128)(2,1)S(...) custom-call(s32[5]{0:T(128)S(1)} %stack.234.scalars, ...), custom_call_target="tpu_custom_call" | custom-call | tf_op jit(solution)/shard_map/attend/pallas_call | solution.py:581
  176.8 14.1 %forward.1 = (bf16[512,3072]{1,0:T(8,128)(2,1)}, bf16[512,3072]{1,0:T(8,128)(2,1)}, f32[512,768]{1,0:T(8,128)S(1)}, f32[512,1]{1,0:T(8,128)S(1)}, bf16[16,2,16,768]{3,2,1,0:T(8,128)(2,1)S(1)}) custom-call(s32[5]{0:T(128)S(1)} %stack.234.scalars, bf16[512,768]{1,0:T(8,128)(2,1)S(1)} %get-tuple-element.45.low_ref, f32[512,768]{1,0:T(8,128)S(1)} %get-tuple-element.46.n_ref, ...), custom_call_target="tpu_custom_call" | custom-call | tf_op jit(solution)/shard_map/forward/pallas_call | solution.py:596
  195.1 5.0 %all-to-all-start = ((bf16[32,16,768]{2,1,0:T(8,128)(2,1)}), bf16[32,16,768]{2,1,0:T(8,128)(2,1)S(1)}, u32[]{:S(2)}, u32[]{:S(2)}) async-start(bf16[32,16,768]{2,1,0:T(8,128)(2,1)} %bitcast.311), calls=%async_computation | async-start | bytes 1572864 | tf_op jit(solution)/shard_map/all_to_all | solution.py:504
  204.3 9.0 %down.1 = (bf16[2,2,2,4,48,768]{5,4,3,2,1,0:T(8,128)(2,1)S(1)}, bf16[2,2,2,4,48,768]{5,4,3,2,1,0:T(8,128)(2,1)}, f32[512,768]{1,0:T(8,128)S(1)}, bf16[512,768]{1,0:T(8,128)(2,1)S(1)}, f32[3,768]{1,0:T(4,128)S(1)}) custom-call(s32[5]{0:T(128)S(1)} %copy-done.45, bf16[16,2,16,768]{3,2,1,0:T(8,128)(2,1)} %bitcast.56.cot_ref, f32[512,768]{1,0:T(8,128)S(1)} %copy-done.28, ...), custom_call_target="tpu_custom_call" | custom-call | tf_op jit(solution)/shard_map/down/pallas_call | solution.py:612
  217.7 25.6 %up.1 = (f32[512,768]{1,0:T(8,128)}, bf16[512,768]{1,0:T(8,128)(2,1)}, f32[3,768]{1,0:T(4,128)S(1)}, f32[1,3072]{1,0:T(1,128)S(1)}, bf16[2,2,2,4,48,768]{5,4,3,2...) custom-call(s32[5]{0:T(128)S(1)} %copy-done.45, bf16[512,768]{1,0:T(8,128)(2,1)} %copy-done.30, ...), custom_call_target="tpu_custom_call" | custom-call | tf_op jit(solution)/shard_map/up/pallas_call | solution.py:622
  243.3 29.4 %attend_back.1 = (bf16[2,256,768]{2,1,0:T(8,128)(2,1)S(1)}, f32[2,768]{1,0:T(2,128)S(1)}, bf16[2,2,2,4,48,768]{5,4,3,2,1,0:T(8,128)(2,1)}, bf16[2,2,2,4,48,768]{5,4,3,2,1,0:T(8,128)(2,1)}) custom-call(s32[5]{0:T(128)S(1)} %copy-done.45, bf16[512,768]{1,0:T(8,128)(2,1)} %get-tuple-element.55.gattn_ref, f32[512,768]{1,0:T(8,128)} %get-tuple-element.56.first_ref, ...), custom_call_target="tpu_custom_call" | custom-call | tf_op jit(solution)/shard_map/attend_back/pallas_call | solution.py:636
  276.4 5.8 %all-to-all-start.1 = ((bf16[16,32,768]{2,1,0:T(8,128)(2,1)}), bf16[16,32,768]{2,1,0:T(8,128)(2,1)S(1)}, u32[]{:S(2)}, u32[]{:S(2)}) async-start(bf16[16,32,768]{2,1,0:T(8,128)(2,1)} %bitcast.48), calls=%async_computation.1 | async-start | bytes 1572864 | tf_op jit(solution)/shard_map/all_to_all | solution.py:506
  297.1 4.5 %collective-permute-start.58 = (f32[12,768]{1,0:T(8,128)S(1)}, f32[12,768]{1,0:T(8,128)S(1)}, u32[]{:S(2)}, u32[]{:S(2)}) collective-permute-start(f32[12,768]{1,0:T(8,128)S(1)} %add.221), channel_id=1, source_target_pairs={{0,16},{1,17},{2,18},{3,19},{4,20},{5,21},{6,22},{7,23},{8,24},{9,... | collective-permute-start | bytes 110600 | tf_op jit(solution)/shard_map/ppermute | solution.py:40
  332.8 7.0 %collective-permute-done.41 = bf16[2,4,48,768]{3,2,1,0:T(8,128)(2,1)S(1)} collective-permute-done((bf16[2,4,48,768]{3,2,1,0:T(8,128)(2,1)S(1)}, bf16[2,4,48,768]{3,2,1,0:T(8,128)(2,1)S(1)}, u32[]{:S(2)}, u32[]{:S(2)}) %collective-permute-start.41) | collective-permute-done | bytes 589856 | tf_op jit(solution)/shard_map/ppermute | solution.py:40
  345.4 7.0 %collective-permute-done.48 = bf16[2,4,48,768]{3,2,1,0:T(8,128)(2,1)S(1)} collective-permute-done((bf16[2,4,48,768]{3,2,1,0:T(8,128)(2,1)S(1)}, bf16[2,4,48,768]{3,2,1,0:T(8,128)(2,1)S(1)}, u32[]{:S(2)}, u32[]{:S(2)}) %collective-permute-start.48) | collective-permute-done | bytes 589856 | tf_op jit(solution)/shard_map/ppermute | solution.py:40
  358.1 4.2 %collective-permute-done.35 = bf16[4,48,768]{2,1,0:T(8,128)(2,1)S(1)} collective-permute-done((bf16[4,48,768]{2,1,0:T(8,128)(2,1)S(1)}, bf16[4,48,768]{2,1,0:T(8,128)(2,1)S(1)}, u32[]{:S(2)}, u32[]{:S(2)}) %collective-permute-start.35) | collective-permute-done | bytes 294944 | tf_op jit(solution)/shard_map/ppermute | solution.py:40
  364.1 4.5 %collective-permute-done.42 = bf16[4,48,768]{2,1,0:T(8,128)(2,1)S(1)} collective-permute-done((bf16[4,48,768]{2,1,0:T(8,128)(2,1)S(1)}, bf16[4,48,768]{2,1,0:T(8,128)(2,1)S(1)}, u32[]{:S(2)}, u32[]{:S(2)}) %collective-permute-start.42) | collective-permute-done | bytes 294944 | tf_op jit(solution)/shard_map/ppermute | solution.py:40
  369.0 4.1 %collective-permute-done.49 = bf16[4,48,768]{2,1,0:T(8,128)(2,1)S(1)} collective-permute-done((bf16[4,48,768]{2,1,0:T(8,128)(2,1)S(1)}, bf16[4,48,768]{2,1,0:T(8,128)(2,1)S(1)}, u32[]{:S(2)}, u32[]{:S(2)}) %collective-permute-start.49) | collective-permute-done | bytes 294944 | tf_op jit(solution)/shard_map/ppermute | solution.py:40
  374.3 10.2 %collective-permute-done.45 = bf16[2,2,48,768]{3,2,0,1:T(8,128)(2,1)S(1)} collective-permute-done((bf16[2,2,48,768]{3,2,0,1:T(8,128)(2,1)S(1)}, bf16[2,2,48,768]{3,2,0,1:T(8,128)(2,1)S(1)}, u32[]{:S(2)}, u32[]{:S(2)}) %collective-permute-start.45) | collective-permute-done | bytes 294944 | tf_op jit(solution)/shard_map/ppermute | solution.py:40
  389.1 6.9 %collective-permute-done.46 = bf16[2,48,768]{2,1,0:T(8,128)(2,1)S(1)} collective-permute-done((bf16[2,48,768]{2,1,0:T(8,128)(2,1)S(1)}, bf16[2,48,768]{2,1,0:T(8,128)(2,1)S(1)}, u32[]{:S(2)}, u32[]{:S(2)}) %collective-permute-start.46) | collective-permute-done | bytes 147488 | tf_op jit(solution)/shard_map/ppermute | solution.py:40
  (355 shorter events, 156.1 us)
Async XLA Ops:
  6.8 28.0 %collective-permute-start.12 = (bf16[2,48,768]{2,1,0:T(8,128)(2,1)S(1)}, bf16[2,48,768]{2,1,0:T(8,128)(2,1)S(1)}, u32[]{:S(2)}, u32[]{:S(2)}) collective-permute-start(bf16[2,48,768]{2,1,0:T(8,128)(2,1)S(1)} %pad_maximum_fusion.20), channel_id=1, source_target_pairs={{0,16},{1,17},{2,18},{3,19},{4,20},{5,21},{6,22},{7,23},{8,24},{9,... | collective-permute-start | bytes 442376 | tf_op jit(solution)/shard_map/ppermute | solution.py:40
  10.8 90.6 %all-to-all-start.2 = ((bf16[16,32,768]{2,1,0:T(8,128)(2,1)}), bf16[16,32,768]{2,1,0:T(8,128)(2,1)S(1)}, u32[]{:S(2)}, u32[]{:S(2)}) async-start(bf16[16,32,768]{2,1,0:T(8,128)(2,1)} %bitcast.54), calls=%async_computation.2 | async-start | bytes 1572864 | tf_op jit(solution)/shard_map/all_to_all | solution.py:496
  61.1 34.6 %collective-permute-start.5 = (bf16[2,4,48,768]{3,2,1,0:T(8,128)(2,1)S(1)}, bf16[2,4,48,768]{3,2,1,0:T(8,128)(2,1)S(1)}, u32[]{:S(2)}, u32[]{:S(2)}) collective-permute-start(bf16[2,4,48,768]{3,2,1,0:T(8,128)(2,1)S(1)} %pad_maximum_fusion.2.refs_0_), channel_id=1, source_target_pairs={{0,2},{1,3},{2,0},{3,1},{4,6},{5,7},{6,4},{7,5},{8,10},{9,11},{10,... | collective-permute-start | bytes 1769480 | tf_op jit(solution)/shard_map/ppermute | solution.py:40
  61.9 36.2 %collective-permute-start.6 = (bf16[2,4,48,768]{3,2,1,0:T(8,128)(2,1)S(1)}, bf16[2,4,48,768]{3,2,1,0:T(8,128)(2,1)}, u32[]{:S(2)}, u32[]{:S(2)}) collective-permute-start(bf16[2,4,48,768]{3,2,1,0:T(8,128)(2,1)S(1)} %pad_maximum_fusion.2.refs_0_), channel_id=1, source_target_pairs={{0,1},{1,0},{2,3},{3,2},{4,5},{5,4},{6,7},{7,6},{8,9},{9,8},{10,11... | collective-permute-start | bytes 1769480 | tf_op jit(solution)/shard_map/ppermute | solution.py:40
  66.2 32.1 %collective-permute-start.9 = (bf16[2,4,48,768]{3,2,1,0:T(8,128)(2,1)S(1)}, bf16[2,4,48,768]{3,2,1,0:T(8,128)(2,1)S(1)}, u32[]{:S(2)}, u32[]{:S(2)}) collective-permute-start(bf16[2,4,48,768]{3,2,1,0:T(8,128)(2,1)S(1)} %pad_maximum_fusion.3.refs_4_), channel_id=1, source_target_pairs={{0,2},{1,3},{2,0},{3,1},{4,6},{5,7},{6,4},{7,5},{8,10},{9,11},{10,... | collective-permute-start | bytes 1769480 | tf_op jit(solution)/shard_map/ppermute | solution.py:40
  68.7 26.9 %collective-permute-start = (bf16[256,768]{1,0:T(8,128)(2,1)S(1)}, bf16[256,768]{1,0:T(8,128)(2,1)S(1)}, u32[]{:S(2)}, u32[]{:S(2)}) collective-permute-start(bf16[256,768]{1,0:T(8,128)(2,1)S(1)} %dynamic-slice_bitcast_fusion.1), channel_id=1, source_target_pairs={{0,1},{1,0},{2,3},{3,2},{4,5},{5,4},{6,7},{7,6},{8,9},{9,8},{10,11... | collective-permute-start | bytes 1179656 | tf_op jit(solution)/shard_map/ppermute | solution.py:40
  99.1 31.3 %collective-permute-start.20 = (bf16[2,4,48,768]{3,2,1,0:T(8,128)(2,1)S(1)}, bf16[2,4,48,768]{3,2,1,0:T(8,128)(2,1)}, u32[]{:S(2)}, u32[]{:S(2)}) collective-permute-start(bf16[2,4,48,768]{3,2,1,0:T(8,128)(2,1)S(1)} %pad_maximum_fusion.5.refs_4_), channel_id=1, source_target_pairs={{0,4},{1,5},{2,6},{3,7},{4,0},{5,1},{6,2},{7,3},{8,12},{9,13},{10,... | collective-permute-start | bytes 1769480 | tf_op jit(solution)/shard_map/ppermute | solution.py:40
  103.0 92.1 %all-to-all-start.3 = ((bf16[32,16,768]{2,1,0:T(8,128)(2,1)}), bf16[32,16,768]{2,1,0:T(8,128)(2,1)}, u32[]{:S(2)}, u32[]{:S(2)}) async-start(bf16[32,16,768]{2,1,0:T(8,128)(2,1)} %pick.3), calls=%async_computation.3 | async-start | bytes 1572864 | tf_op jit(solution)/shard_map/all_to_all | solution.py:498
  114.7 28.4 %collective-permute-start.30 = (bf16[2,4,48,768]{3,2,1,0:T(8,128)(2,1)}, bf16[2,4,48,768]{3,2,1,0:T(8,128)(2,1)}, u32[]{:S(2)}, u32[]{:S(2)}) collective-permute-start(bf16[2,4,48,768]{3,2,1,0:T(8,128)(2,1)} %pad_maximum_fusion.7.refs_12_), channel_id=1, source_target_pairs={{0,4},{1,5},{2,6},{3,7},{4,0},{5,1},{6,2},{7,3},{8,12},{9,13},{10,... | collective-permute-start | bytes 1769480 | tf_op jit(solution)/shard_map/ppermute | solution.py:40
  118.0 25.2 %collective-permute-start.7 = (bf16[2,4,48,768]{3,2,1,0:T(8,128)(2,1)}, bf16[2,4,48,768]{3,2,1,0:T(8,128)(2,1)}, u32[]{:S(2)}, u32[]{:S(2)}) collective-permute-start(bf16[2,4,48,768]{3,2,1,0:T(8,128)(2,1)} %collective-permute-done.6.refs_2_), channel_id=1, source_target_pairs={{0,2},{1,3},{2,0},{3,1},{4,6},{5,7},{6,4},{7,5},{8,10},{9,11},{10,... | collective-permute-start | bytes 1769480 | tf_op jit(solution)/shard_map/ppermute | solution.py:40
  132.6 44.1 %collective-permute-start.29 = (bf16[2,4,48,768]{3,2,1,0:T(8,128)(2,1)}, bf16[2,4,48,768]{3,2,1,0:T(8,128)(2,1)}, u32[]{:S(2)}, u32[]{:S(2)}) collective-permute-start(bf16[2,4,48,768]{3,2,1,0:T(8,128)(2,1)} %pad_maximum_fusion.7.refs_12_), channel_id=1, source_target_pairs={{0,2},{1,3},{2,0},{3,1},{4,6},{5,7},{6,4},{7,5},{8,10},{9,11},{10,... | collective-permute-start | bytes 1769480 | tf_op jit(solution)/shard_map/ppermute | solution.py:40
  133.9 42.9 %collective-permute-start.17 = (bf16[2,4,48,768]{3,2,1,0:T(8,128)(2,1)}, bf16[2,4,48,768]{3,2,1,0:T(8,128)(2,1)}, u32[]{:S(2)}, u32[]{:S(2)}) collective-permute-start(bf16[2,4,48,768]{3,2,1,0:T(8,128)(2,1)} %collective-permute-done.16.refs_2_), channel_id=1, source_target_pairs={{0,2},{1,3},{2,0},{3,1},{4,6},{5,7},{6,4},{7,5},{8,10},{9,11},{10,... | collective-permute-start | bytes 1769480 | tf_op jit(solution)/shard_map/ppermute | solution.py:40
  143.1 33.6 %collective-permute-start.21 = (bf16[2,4,48,768]{3,2,1,0:T(8,128)(2,1)}, bf16[2,4,48,768]{3,2,1,0:T(8,128)(2,1)}, u32[]{:S(2)}, u32[]{:S(2)}) collective-permute-start(bf16[2,4,48,768]{3,2,1,0:T(8,128)(2,1)} %collective-permute-done.20.refs_6_), channel_id=1, source_target_pairs={{0,2},{1,3},{2,0},{3,1},{4,6},{5,7},{6,4},{7,5},{8,10},{9,11},{10,... | collective-permute-start | bytes 1769480 | tf_op jit(solution)/shard_map/ppermute | solution.py:40
  143.1 33.6 %collective-permute-start.27 = (bf16[2,4,48,768]{3,2,1,0:T(8,128)(2,1)}, bf16[2,4,48,768]{3,2,1,0:T(8,128)(2,1)}, u32[]{:S(2)}, u32[]{:S(2)}) collective-permute-start(bf16[2,4,48,768]{3,2,1,0:T(8,128)(2,1)} %collective-permute-done.26.refs_10_), channel_id=1, source_target_pairs={{0,2},{1,3},{2,0},{3,1},{4,6},{5,7},{6,4},{7,5},{8,10},{9,11},{10,... | collective-permute-start | bytes 1769480 | tf_op jit(solution)/shard_map/ppermute | solution.py:40
  143.6 33.1 %collective-permute-start.31 = (bf16[2,4,48,768]{3,2,1,0:T(8,128)(2,1)}, bf16[2,4,48,768]{3,2,1,0:T(8,128)(2,1)}, u32[]{:S(2)}, u32[]{:S(2)}) collective-permute-start(bf16[2,4,48,768]{3,2,1,0:T(8,128)(2,1)} %collective-permute-done.30.refs_14_), channel_id=1, source_target_pairs={{0,2},{1,3},{2,0},{3,1},{4,6},{5,7},{6,4},{7,5},{8,10},{9,11},{10,... | collective-permute-start | bytes 1769480 | tf_op jit(solution)/shard_map/ppermute | solution.py:40
  195.1 79.6 %all-to-all-start = ((bf16[32,16,768]{2,1,0:T(8,128)(2,1)}), bf16[32,16,768]{2,1,0:T(8,128)(2,1)S(1)}, u32[]{:S(2)}, u32[]{:S(2)}) async-start(bf16[32,16,768]{2,1,0:T(8,128)(2,1)} %bitcast.311), calls=%async_computation | async-start | bytes 1572864 | tf_op jit(solution)/shard_map/all_to_all | solution.py:504
  272.8 35.1 %collective-permute-start.33 = (bf16[2,2,2,4,48,768]{5,4,3,2,1,0:T(8,128)(2,1)}, bf16[2,2,2,4,48,768]{5,4,3,2,1,0:T(8,128)(2,1)}, u32[]{:S(2)}, u32[]{:S(2)}) collective-permute-start(bf16[2,2,2,4,48,768]{5,4,3,2,1,0:T(8,128)(2,1)} %get-tuple-element.64), channel_id=1, source_target_pairs={{0,2},{1,3},{2,0},{3,1},{4,6},{5,7},{6,4},{7,5},{8,10},{9,11},{10,... | collective-permute-start | bytes 7077896 | tf_op jit(solution)/shard_map/ppermute | solution.py:40
  273.0 43.5 %collective-permute-start.40 = (bf16[2,2,2,4,48,768]{5,4,3,2,1,0:T(8,128)(2,1)}, bf16[2,2,2,4,48,768]{5,4,3,2,1,0:T(8,128)(2,1)}, u32[]{:S(2)}, u32[]{:S(2)}) collective-permute-start(bf16[2,2,2,4,48,768]{5,4,3,2,1,0:T(8,128)(2,1)} %get-tuple-element.66), channel_id=1, source_target_pairs={{0,2},{1,3},{2,0},{3,1},{4,6},{5,7},{6,4},{7,5},{8,10},{9,11},{10,... | collective-permute-start | bytes 7077896 | tf_op jit(solution)/shard_map/ppermute | solution.py:40
  273.4 46.7 %collective-permute-start.47 = (bf16[2,2,2,4,48,768]{5,4,3,2,1,0:T(8,128)(2,1)}, bf16[2,2,2,4,48,768]{5,4,3,2,1,0:T(8,128)(2,1)}, u32[]{:S(2)}, u32[]{:S(2)}) collective-permute-start(bf16[2,2,2,4,48,768]{5,4,3,2,1,0:T(8,128)(2,1)} %get-tuple-element.68), channel_id=1, source_target_pairs={{0,2},{1,3},{2,0},{3,1},{4,6},{5,7},{6,4},{7,5},{8,10},{9,11},{10,... | collective-permute-start | bytes 7077896 | tf_op jit(solution)/shard_map/ppermute | solution.py:40
  276.4 37.0 %all-to-all-start.1 = ((bf16[16,32,768]{2,1,0:T(8,128)(2,1)}), bf16[16,32,768]{2,1,0:T(8,128)(2,1)S(1)}, u32[]{:S(2)}, u32[]{:S(2)}) async-start(bf16[16,32,768]{2,1,0:T(8,128)(2,1)} %bitcast.48), calls=%async_computation.1 | async-start | bytes 1572864 | tf_op jit(solution)/shard_map/all_to_all | solution.py:506
  322.3 30.1 %collective-permute-start.48 = (bf16[2,4,48,768]{3,2,1,0:T(8,128)(2,1)S(1)}, bf16[2,4,48,768]{3,2,1,0:T(8,128)(2,1)S(1)}, u32[]{:S(2)}, u32[]{:S(2)}) collective-permute-start(bf16[2,4,48,768]{3,2,1,0:T(8,128)(2,1)S(1)} %get-tuple-element.82), channel_id=1, source_target_pairs={{0,4},{1,5},{2,6},{3,7},{4,0},{5,1},{6,2},{7,3},{8,12},{9,13},{10,... | collective-permute-start | bytes 1769480 | tf_op jit(solution)/shard_map/ppermute | solution.py:40
  327.3 28.7 %collective-permute-start.50 = (bf16[2,4,48,768]{3,2,1,0:T(8,128)(2,1)S(1)}, bf16[2,4,48,768]{3,2,1,0:T(8,128)(2,1)S(1)}, u32[]{:S(2)}, u32[]{:S(2)}) collective-permute-start(bf16[2,4,48,768]{3,2,1,0:T(8,128)(2,1)S(1)} %get-tuple-element.80), channel_id=1, source_target_pairs={{0,1},{1,0},{2,3},{3,2},{4,5},{5,4},{6,7},{7,6},{8,9},{9,8},{10,11... | collective-permute-start | bytes 1769480 | tf_op jit(solution)/shard_map/ppermute | solution.py:40
  330.7 31.6 %collective-permute-start.35 = (bf16[4,48,768]{2,1,0:T(8,128)(2,1)S(1)}, bf16[4,48,768]{2,1,0:T(8,128)(2,1)S(1)}, u32[]{:S(2)}, u32[]{:S(2)}) collective-permute-start(bf16[4,48,768]{2,1,0:T(8,128)(2,1)S(1)} %fusion.32), channel_id=1, source_target_pairs={{0,1},{1,0},{2,3},{3,2},{4,5},{5,4},{6,7},{7,6},{8,9},{9,8},{10,11... | collective-permute-start | bytes 884744 | tf_op jit(solution)/shard_map/ppermute | solution.py:40
  343.3 25.3 %collective-permute-start.42 = (bf16[4,48,768]{2,1,0:T(8,128)(2,1)S(1)}, bf16[4,48,768]{2,1,0:T(8,128)(2,1)S(1)}, u32[]{:S(2)}, u32[]{:S(2)}) collective-permute-start(bf16[4,48,768]{2,1,0:T(8,128)(2,1)S(1)} %fusion.36), channel_id=1, source_target_pairs={{0,1},{1,0},{2,3},{3,2},{4,5},{5,4},{6,7},{7,6},{8,9},{9,8},{10,11... | collective-permute-start | bytes 884744 | tf_op jit(solution)/shard_map/ppermute | solution.py:40
  (103 other events, 1304.1 us)
